TPU v7x, 128 devices: a whole 4x4x4 slice. The times are simulated.
128 devices in a mesh: grp: 2 (over x_lo), seq: 64 (over z, x_hi, y, core).
Axes of the slice: x: 4 (x_hi: 2, x_lo: 2; x = x_hi * 2 + x_lo), y: 4, z: 4, core: 2. Of those that a mesh axis runs over, the one named last changes fastest.
Arguments:
- feats: bfloat16 [128, 128, 384], P('seq', None, 'grp'), may hold values from -6 to 6
- conv_weight: bfloat16 [3, 128, 128], replicated, may hold values from -0.3125 to 0.3125
- conv_bias: float32 [128], replicated, may hold values from -3 to 3
- latent_projection_weight: bfloat16 [16, 128], replicated, may hold values from -0.75 to 0.75
- noise: bfloat16 [128, 16, 384], P('seq', None, 'grp'), may hold values from -6 to 6
- step_index: int32 [1], replicated, may hold values from 0 to 49
- hist: bfloat16 [512, 64], P('seq'), may hold values from -6 to 6
- hist_level: int32 [512], P('seq'), may hold values from 0 to 2
- hist_count: int32 [64], replicated, may hold values from 1 to 8, 384 in all
- w_in: bfloat16 [64, 3072], replicated, may hold values from -2 to 2
- w_hist: bfloat16 [3, 64, 3072], replicated, may hold values from -0.75 to 0.75
- norm_gain: float32 [3072], replicated, may hold values from 0.5 to 2
- w_query: bfloat16 [3072, 1536], P(None, 'grp'), may hold values from -2 to 2
- w_key: bfloat16 [3072, 1536], P(None, 'grp'), may hold values from -2 to 2
- w_value: bfloat16 [3072, 1536], P(None, 'grp'), may hold values from -0.109375 to 0.109375
- q_gain: float32 [128], replicated, may hold values from 0.5 to 6
- k_gain: float32 [128], replicated, may hold values from 0.5 to 6
- w_out: bfloat16 [1536, 3072], P('grp'), may hold values from -0.5 to 0.5
Outputs:
- attention_out: bfloat16 [12288, 3072], P('seq', 'grp')
Inputs may be any that keep to these rules, and one draw needn't show every extreme that they name: hist_count[s] of the 8 history slots of seq index s are live; the largest count is exactly 8.
All inputs are finite; a program needn't handle non-finite values.
Results may differ from a plain program's by a relative error of at most 0.0095.
The roundings to bfloat16 on the way count: a program that leaves them out, or rounds other values in their place, can miss the bound.
Values may be sent and summed in bfloat16 or wider, within the bound.
A program may use at most 256 MiB of HBM per device.

v0:
```python
import math

import jax
import jax.numpy as jnp
from jax import lax
from jax.sharding import PartitionSpec as P

STEPS = 50


EPSILON = 1e-06


def from_behind(value, axis, steps):
    count = lax.axis_size(axis)
    initial, last = (max(0, -steps), min(count, count - steps))
    return lax.ppermute(value, axis, [(source, source + steps) for source in range(initial, last)])


def time_embed(step_index, width):
    half_width = width // 2
    frequency = jnp.exp(-math.log(10000.0) * jnp.arange(half_width, dtype=jnp.float32) / half_width)
    angles = step_index[0].astype(jnp.float32) * frequency
    return jnp.concatenate([jnp.cos(angles), jnp.sin(angles)])


def rms_scale(values, gain):
    return values * lax.rsqrt(jnp.mean(values * values, axis=-1, keepdims=True) + EPSILON) * gain


def local(
    feats,
    conv_weight,
    conv_bias,
    latent_projection_weight,
    noise,
    step_index,
    hist,
    hist_level,
    hist_count,
    w_in,
    w_hist,
    norm_gain,
    w_query,
    w_key,
    w_value,
    q_gain,
    k_gain,
    w_out,
):
    frame_count, channels, pixels = feats.shape
    earlier = from_behind(feats, "seq", 1)
    padded = jnp.concatenate([earlier, feats], axis=0)
    total = jnp.zeros(feats.shape, jnp.float32)
    for tap_index in range(3):
        window = padded[2 - tap_index : 2 - tap_index + frame_count]
        total = total + jnp.einsum(
            "oc,tcp->top", conv_weight[tap_index], window, preferred_element_type=jnp.float32
        )
    hidden_state = jax.nn.silu(total + conv_bias[None, :, None]).astype(jnp.bfloat16)
    sigma = (STEPS - step_index[0].astype(jnp.float32)) / STEPS
    latent_input = jnp.einsum(
        "qb,zby->zqy", latent_projection_weight, hidden_state, preferred_element_type=jnp.float32
    )
    noisy = ((1.0 - sigma) * latent_input + sigma * noise.astype(jnp.float32)).astype(jnp.bfloat16)
    lat_channels = noisy.shape[1]
    patches = (
        noisy.reshape(frame_count, lat_channels, pixels // 4, 4)
        .transpose(0, 2, 1, 3)
        .reshape(frame_count, pixels // 4, lat_channels * 4)
    )
    width = w_in.shape[1]
    embed = time_embed(step_index, width)
    block_rows = patches.shape[1]
    summed = (
        jnp.dot(patches.reshape(-1, patches.shape[2]), w_in, preferred_element_type=jnp.float32)
        + embed
    )
    tokens = lax.all_gather(
        rms_scale(summed, norm_gain).astype(jnp.bfloat16).reshape(frame_count, block_rows, width),
        "grp",
        axis=1,
        tiled=True,
    ).reshape(-1, width)
    history = jnp.zeros((hist.shape[0], width), jnp.float32)
    for level in range(3):
        history = (
            history
            + jnp.dot(hist, w_hist[level], preferred_element_type=jnp.float32)
            * (hist_level == level).astype(jnp.float32)[:, None]
        )
    history = rms_scale(history, norm_gain).astype(jnp.bfloat16)
    both_rows = jnp.concatenate([tokens, history], axis=0)
    sec_rows = tokens.shape[0]
    key_rows = both_rows.shape[0]
    head_size = q_gain.shape[0]
    heads_local = w_query.shape[1] // head_size
    query = rms_scale(
        jnp.dot(tokens, w_query, preferred_element_type=jnp.float32).reshape(
            sec_rows, heads_local, head_size
        ),
        q_gain,
    ).astype(jnp.bfloat16)
    flattened_keys = (
        rms_scale(
            jnp.dot(both_rows, w_key, preferred_element_type=jnp.float32).reshape(
                key_rows, heads_local, head_size
            ),
            k_gain,
        )
        .astype(jnp.bfloat16)
        .reshape(key_rows, heads_local * head_size)
    )
    values_flat = jnp.dot(both_rows, w_value, preferred_element_type=jnp.float32).astype(
        jnp.bfloat16
    )
    seq_count = lax.axis_size("seq")
    shard_ids = jnp.arange(seq_count, dtype=jnp.int32)
    scale = 1.0 / math.sqrt(head_size)
    run_max = jnp.full((heads_local, sec_rows), -1e30, jnp.float32)
    key_piece = lax.all_gather(flattened_keys, "seq", axis=0, tiled=True)
    value_piece = lax.all_gather(values_flat, "seq", axis=0, tiled=True)
    count_rows = key_piece.shape[0]
    row_index = jnp.arange(count_rows, dtype=jnp.int32)
    owner = row_index // key_rows
    local_index = row_index - owner * key_rows
    owner_count = jnp.sum(
        jnp.where(owner[:, None] == shard_ids[None, :], hist_count[None, :], 0), axis=1
    )
    alive = (local_index < sec_rows) | (local_index - sec_rows < owner_count)
    key_heads = key_piece.reshape(count_rows, heads_local, head_size)
    value_heads = value_piece.reshape(count_rows, heads_local, head_size)
    scores = (
        jnp.einsum("qhd,khd->hqk", query, key_heads, preferred_element_type=jnp.float32) * scale
    )
    scores = jnp.where(alive[None, None, :], scores, -1e30)
    new_max = jnp.maximum(run_max, jnp.max(scores, axis=-1))
    soft = jnp.where(alive[None, None, :], jnp.exp(scores - new_max[..., None]), 0.0)
    new_sum = jnp.sum(soft, axis=-1)
    new_weighted = jnp.einsum(
        "hqk,khd->hqd", soft.astype(jnp.bfloat16), value_heads, preferred_element_type=jnp.float32
    )
    attended = new_weighted / new_sum[..., None]
    heads_out = (
        attended.astype(jnp.bfloat16).transpose(1, 0, 2).reshape(sec_rows, heads_local * head_size)
    )
    partial_out = jnp.dot(heads_out, w_out, preferred_element_type=jnp.float32)
    return lax.psum_scatter(
        partial_out.astype(jnp.bfloat16), "grp", scatter_dimension=1, tiled=True
    )


def solution(mesh):
    placed = (
        P("seq", None, "grp"),
        P(),
        P(),
        P(),
        P("seq", None, "grp"),
        P(),
        P("seq", None),
        P("seq"),
        P(),
        P(),
        P(),
        P(),
        P(None, "grp"),
        P(None, "grp"),
        P(None, "grp"),
        P(),
        P(),
        P("grp", None),
    )
    return jax.shard_map(
        local, mesh=mesh, in_specs=placed, out_specs=P("seq", "grp"), check_vma=False
    )
```

profile of v0, /device:TPU:4, one launch (start us, length us, event | category | flops | bytes accessed | tf_op | source)
XLA Modules:
  0.0 366.7 jit_solution(9510496227103605106)
XLA Ops:
  6.6 2.1 collective-permute-start
  9.4 1.1 fusion.51
  10.4 0.7 compare_convert_fusion
  11.1 1.2 convolution_multiply_fusion.2
  12.3 1.2 fusion.7
  13.5 3.0 collective-permute-done
  16.5 1.0 convolution_add_fusion.2
  17.5 1.1 fusion.24
  18.6 0.1 copy.47
  19.0 0.4 multiply_reduce_fusion
  19.4 1.0 multiply_convert_fusion
  20.5 1.3 multiply_reduce_fusion.2
  21.9 24.3 %all-gather.4.cloned.1.call-done = bf16[2,96,3072]{2,1,0:T(8,128)(2,1)} async-done(((bf16[2,48,3072]{2,1,0:T(8,128)(2,1)}), bf16[2,96,3072]{2,1,0:T(8,128)(2,1)}) %all-gather.4.cloned.1.call-update) | async-done | bytes 1179664 | tf_op jit(solution)/shard_map/all_gather | solution.py:79
  46.2 3.8 %fusion.67 = (f32[200,768]{1,0:T(8,128)S(1)}, f32[200,768]{1,0:T(8,128)S(1)}) fusion(bf16[3072,768]{1,0:T(8,128)(2,1)} %param.31, bf16[8,3072]{1,0:T(8,128)(2,1)S(1)} %multiply_convert_fusion.4, bf16[192,3072]{1,0:T(8,128)(2,1)} %bitcast.98), kind=kOutput, calls=%fused_computation.95 | convolution fusion | flops 946329600 | bytes 7176192 | tf_op jit(solution)/shard_map/dot_general | solution.py:106
  50.1 0.3 reduce_sum.58
  50.5 0.1 copy.51
  50.6 0.3 mul.186
  50.9 0.9 fusion.27
  51.9 4.6 %convolution_convert_fusion.1 = bf16[200,768]{1,0:T(8,128)(2,1)} fusion(bf16[3072,768]{1,0:T(8,128)(2,1)} %param.32, bf16[8,3072]{1,0:T(8,128)(2,1)S(1)} %multiply_convert_fusion.4, bf16[192,3072]{1,0:T(8,128)(2,1)} %bitcast.99), kind=kOutput, calls=%fused_computation.18 | convolution fusion | flops 946329600 | bytes 6254592 | tf_op jit(solution)/shard_map/dot_general | solution.py:114
  56.5 0.2 reduce-scatter.2.cloned.1.call-start
  56.7 6.7 %copy.49 = bf16[3072,768]{0,1:T(8,128)(2,1)} copy(bf16[3072,768]{1,0:T(8,128)(2,1)} %param.30) | data formatting | bytes 9437184 | tf_op args[12]
  63.5 0.6 select_reduce_fusion
  64.1 4.3 %multiply_reduce_fusion.1 = (f32[192,6]{0,1:T(8,128)S(1)}, f32[192,6,128]{2,0,1:T(8,128)S(1)}) fusion(bf16[192,3072,1]{1,0,2:T(8,128)(2,1)S(1)} %bitcast.100, bf16[6,128,3072]{2,1,0:T(8,128)(2,1)} %bitcast.93), kind=kOutput, calls=%fused_computation.37 | convolution fusion | flops 906263424 | bytes 6492672 | tf_op jit(solution)/shard_map/dot_general | solution.py:99
  68.5 96.6 %all-gather.6.cloned.1.call-done = bf16[12800,768]{1,0:T(8,128)(2,1)} async-done(((bf16[200,768]{1,0:T(8,128)(2,1)}), bf16[12800,768]{1,0:T(8,128)(2,1)}) %all-gather.6.cloned.1.call-update) | async-done | bytes 19660816 | tf_op jit(solution)/shard_map/all_gather | solution.py:121
  165.1 23.8 %copy.52 = bf16[12800,768]{0,1:T(8,128)(2,1)} copy(bf16[12800,768]{1,0:T(8,128)(2,1)} %all-gather.6.cloned.1.call-done) | data formatting | bytes 39321600 | tf_op jit(solution)/shard_map/all_gather | solution.py:121
  189.0 27.5 %fusion = (f32[6,192]{1,0:T(8,128)S(1)}, f32[6,192,12800]{2,1,0:T(8,128)}) fusion(pred[12800]{0:T(1024)(128)(4,1)S(1)} %fusion.46, bf16[12800,6,128]{0,2,1:T(8,128)(2,1)} %bitcast.91, f32[192,6,128]{2,0,1:T(8,128)S(1)} %get-tuple-element.15, f32[128]{0:T(128)S(1)} %copy-done.4, f32[192,6]{0,1:T(8,128)S(1)} %add_rsqrt_fusion.1), kind=kOutput, calls=%fused_computation.2 | convolution fusion | flops 3819551744 | bytes 79255552 | tf_op jit(solution)/shard_map/qhd,khd->hqk/dot_general | solution.py:134
  216.5 21.4 %fusion.1 = f32[6,192]{1,0:T(8,128)S(1)} fusion(f32[6,192,12800]{2,1,0:T(8,128)} %get-tuple-element.17, f32[6,192]{1,0:T(8,128)S(1)} %broadcast_maximum_fusion, pred[12800]{0:T(1024)(128)(4,1)S(1)} %fusion.46), kind=kLoop, calls=%fused_computation.3 | loop fusion | flops 73726848 | bytes 59004416 | tf_op jit(solution)/shard_map/reduce_sum | solution.py:139
  237.9 42.6 %all-gather.8.cloned.1.call-done = bf16[12800,768]{1,0:T(8,128)(2,1)} async-done(((bf16[200,768]{1,0:T(8,128)(2,1)}), bf16[12800,768]{1,0:T(8,128)(2,1)}) %all-gather.8.cloned.1.call-update) | async-done | bytes 19660816 | tf_op jit(solution)/shard_map/all_gather | solution.py:122
  280.5 23.8 %copy.54 = bf16[12800,768]{0,1:T(8,128)(2,1)} copy(bf16[12800,768]{1,0:T(8,128)(2,1)} %all-gather.8.cloned.1.call-done) | data formatting | bytes 39321600 | tf_op jit(solution)/shard_map/all_gather | solution.py:122
  304.3 27.1 %fusion.17 = bf16[6,24,8,128]{3,2,1,0:T(8,128)(2,1)S(1)} fusion(bf16[12800,6,128]{0,2,1:T(8,128)(2,1)} %bitcast.92, f32[6,192,12800]{2,1,0:T(8,128)} %get-tuple-element.17, f32[6,192]{1,0:T(8,128)S(1)} %broadcast_maximum_fusion, pred[12800]{0:T(1024)(128)(4,1)S(1)} %fusion.46, f32[192,6]{0,1:T(8,128)S(1)} %bitcast.97), kind=kOutput, calls=%fused_computation.23 | convolution fusion | flops 3848896512 | bytes 78960128 | tf_op jit(solution)/shard_map/hqk,khd->hqd/dot_general | solution.py:140
  331.3 4.5 %convolution_convert_fusion = bf16[192,3072]{1,0:T(8,128)(2,1)} fusion(bf16[768,3072]{1,0:T(8,128)(2,1)} %param.35, bf16[6,24,8,128]{3,2,1,0:T(8,128)(2,1)S(1)} %fusion.17), kind=kOutput, calls=%fused_computation.7 | convolution fusion | flops 906559488 | bytes 6193152 | tf_op jit(solution)/shard_map/dot_general | solution.py:147
  335.8 24.3 %reduce-scatter.2.cloned.1.call-done = bf16[192,1536]{1,0:T(8,128)(2,1)} async-done(((bf16[192,3072]{1,0:T(8,128)(2,1)}), bf16[192,1536]{1,0:T(8,128)(2,1)}) %reduce-scatter.2.cloned.1.call-update) | async-done | bytes 589840 | tf_op jit(solution)/shard_map/reduce_scatter | solution.py:148
  (38 shorter events, 0.8 us)
Async XLA Ops:
  6.5 12.4 %copy-start = (bf16[64,3072]{1,0:T(8,128)(2,1)S(1)}, bf16[64,3072]{1,0:T(8,128)(2,1)}, u32[]{:S(2)}) copy-start(bf16[64,3072]{1,0:T(8,128)(2,1)} %param.27) | copy-start | bytes 1179652
  6.5 13.9 %copy-start.3 = (bf16[8,64]{1,0:T(8,128)(2,1)S(1)}, bf16[8,64]{1,0:T(8,128)(2,1)}, u32[]{:S(2)}) copy-start(bf16[8,64]{1,0:T(8,128)(2,1)} %param.24) | copy-start | bytes 3076
  6.5 12.8 %copy-start.2 = (f32[3072]{0:T(1024)S(1)}, f32[3072]{0:T(1024)}, u32[]{:S(2)}) copy-start(f32[3072]{0:T(1024)} %param.29) | copy-start | bytes 36868
  6.5 15.2 %copy-start.6 = (f32[128]{0:T(128)S(1)}, f32[128]{0:T(128)}, u32[]{:S(2)}) copy-start(f32[128]{0:T(128)} %param.34) | copy-start | bytes 1540
  6.5 39.6 %all-gather.4.cloned.1.call-start = ((), (), s32[]{:S(2)}) async-start(), calls=%async_computation.1 | async-start | bytes 1769472 | tf_op jit(solution)/shard_map/all_gather | solution.py:79
  6.6 9.9 %collective-permute-start = (bf16[2,128,192]{1,2,0:T(8,128)(2,1)}, bf16[2,128,192]{1,2,0:T(8,128)(2,1)S(1)}, u32[]{:S(2)}, u32[]{:S(2)}) collective-permute-start(bf16[2,128,192]{1,2,0:T(8,128)(2,1)} %param.18), channel_id=1, source_target_pairs={{0,1},{1,2},{2,3},{3,4},{4,5},{5,6},{6,7},{7,8},{8,9},{9,10},{10,1... | collective-permute-start | bytes 294920 | tf_op jit(solution)/shard_map/ppermute | solution.py:17
  20.4 144.7 %all-gather.6.cloned.1.call-start = ((), (), s32[]{:S(2)}) async-start(), calls=%async_computation.2 | async-start | bytes 19968000 | tf_op jit(solution)/shard_map/all_gather | solution.py:121
  51.8 228.6 %all-gather.8.cloned.1.call-start = ((), (), s32[]{:S(2)}) async-start(), calls=%async_computation.3 | async-start | bytes 19968000 | tf_op jit(solution)/shard_map/all_gather | solution.py:122
  56.5 7.0 %copy-start.5 = (s32[64]{0:T(128)S(1)}, s32[64]{0:T(128)}, u32[]{:S(2)}) copy-start(s32[64]{0:T(128)} %param.26) | copy-start | bytes 772
  56.5 7.6 %copy-start.7 = (bf16[2,96,3072]{2,1,0:T(8,128)(2,1)S(1)}, bf16[2,96,3072]{2,1,0:T(8,128)(2,1)}, u32[]{:S(2)}) copy-start(bf16[2,96,3072]{2,1,0:T(8,128)(2,1)} %all-gather.4.cloned.1.call-done) | copy-start | bytes 3538948
  56.5 303.7 %reduce-scatter.2.cloned.1.call-start = ((), (), s32[]{:S(2)}) async-start(), calls=%async_computation.4 | async-start | bytes 1769472 | tf_op jit(solution)/shard_map/reduce_scatter | solution.py:148
  68.4 120.5 %copy-start.4 = (f32[128]{0:T(128)S(1)}, f32[128]{0:T(128)}, u32[]{:S(2)}) copy-start(f32[128]{0:T(128)} %param.33) | copy-start | bytes 1540
  304.3 55.9 %copy-start.1 = (bf16[64,3072]{1,0:T(8,128)(2,1)S(1)}, bf16[64,3072]{1,0:T(8,128)(2,1)}, u32[]{:S(2)}) copy-start(bf16[64,3072]{1,0:T(8,128)(2,1)} %param.27) | copy-start | bytes 1179652
Sparse Core Ops, SparseCore 0:
  20.5 25.5 all-gather.3
  52.0 113.0 all-gather.5
  168.3 112.1 all-gather.7
  335.9 24.1 reduce-scatter.1
where the time goes:
time: 370 us; the launch traced here: 367 us
  waiting for transfers between devices  191 us (52%)
  matrix products  78.9 us (21%)
  local copies, waits for them, and re-layouts  55.3 us (15%)
  other arithmetic  25 us (7%)
  between operations  14 us (4%)
    all_gather x1, waiting for transfers between devices, local(): key_piece = lax.all_gather(flattened_keys, 'seq', axis=0, tiled=True)  96.6 us
    all_gather x1, waiting for transfers between devices, local(): value_piece = lax.all_gather(values_flat, 'seq', axis=0, tiled=True)  42.6 us
    dot_general x1, matrix products, local(): jnp.einsum('qhd,khd->hqk', query, key_heads, preferred_element_type=jnp.f...  27.5 us
    dot_general x1, matrix products, local(): jnp.einsum('hqk,khd->hqd', soft.astype(jnp.bfloat16), value_heads, prefer...  27.1 us
    reduce_scatter x1, waiting for transfers between devices, local(): lax.psum_scatter(partial_out.astype(jnp.bfloat16), 'grp', scatter_dimensi...  24.3 us
    all_gather x1, waiting for transfers between devices, local(): lax.all_gather(rms_scale(summed, norm_gain).astype(jnp.bfloat16).reshape(...  24.3 us
    all_gather x1, local copies, waits for them, and re-layouts, local(): key_piece = lax.all_gather(flattened_keys, 'seq', axis=0, tiled=True)  23.8 us
    all_gather x1, local copies, waits for them, and re-layouts, local(): value_piece = lax.all_gather(values_flat, 'seq', axis=0, tiled=True)  23.8 us
  transfers between devices with their start and end apart: 5, of which 5 were waited for; matrix products, arithmetic and copies ran while one was open for 26% of the time, Pallas kernels for 0%

commit v1 on v0

v1 whole, which is shorter than its diff:
```python
import functools
import math

import jax
import jax.numpy as jnp
from jax import lax
from jax.experimental import pallas as pl
from jax.experimental.pallas import tpu as pltpu
from jax.sharding import PartitionSpec as P

STEPS = 50
EPSILON = 1e-06
LOG2E = math.log2(math.e)
MESH = pl.DeviceIdType.MESH
BF = jnp.bfloat16
F32 = jnp.float32
HIGH = lax.Precision.HIGHEST
SPAN = 70.0 * LOG2E
SAFE = 75.0 * LOG2E


def time_embed(step_index, width):
    half_width = width // 2
    frequency = jnp.exp(-math.log(10000.0) * jnp.arange(half_width, dtype=F32) / half_width)
    angles = step_index[0].astype(F32) * frequency
    return jnp.concatenate([jnp.cos(angles), jnp.sin(angles)])


def rms_scale(values, gain):
    return values * lax.rsqrt(jnp.mean(values * values, axis=-1, keepdims=True) + EPSILON) * gain


def split(x):
    hi = x.astype(BF)
    return hi, (x - hi.astype(F32)).astype(BF)


def swap(value):
    return lax.ppermute(value, "grp", [(0, 1), (1, 0)])


def gather_kernel(chips, x_ref, out_ref, send_sem, recv_sem, fsend_sem, frecv_sem, local_sem):
    grp = lax.axis_index("grp")
    seq = lax.axis_index("seq")
    core = seq % 2
    chip = seq // 2
    sibling = chip * 2 + 1 - core

    barrier = pltpu.get_barrier_semaphore()
    pl.semaphore_signal(barrier, inc=1, device_id=(grp, sibling), device_id_type=MESH)

    @pl.loop(1, chips)
    def _(k):
        there = ((chip + k) % chips) * 2 + core
        pl.semaphore_signal(barrier, inc=1, device_id=(grp, there), device_id_type=MESH)

    pl.semaphore_wait(barrier, chips)

    def direct(k):
        there = ((chip + k) % chips) * 2 + core
        return pltpu.make_async_remote_copy(
            src_ref=x_ref, dst_ref=out_ref.at[seq], send_sem=send_sem.at[k], recv_sem=recv_sem.at[k],
            device_id=(grp, there), device_id_type=MESH)

    def forward(k):
        source = ((chip - k + chips) % chips) * 2 + core
        return pltpu.make_async_remote_copy(
            src_ref=out_ref.at[source], dst_ref=out_ref.at[source], send_sem=fsend_sem.at[k], recv_sem=frecv_sem.at[k],
            device_id=(grp, sibling), device_id_type=MESH)

    @pl.loop(1, chips)
    def _(k):
        direct(k).start()

    own = pltpu.make_async_copy(x_ref, out_ref.at[seq], local_sem)
    own.start()
    own.wait()
    forward(0).start()

    @pl.loop(1, chips)
    def _(k):
        direct(k).wait_recv()
        forward(k).start()

    @pl.loop(0, chips)
    def _(k):
        forward(k).wait_recv()
        forward(k).wait_send()

    @pl.loop(1, chips)
    def _(k):
        direct(k).wait_send()


def gather_blocks(x, count, ident):
    chips = count // 2
    return pl.pallas_call(
        functools.partial(gather_kernel, chips),
        out_shape=jax.ShapeDtypeStruct((count,) + x.shape, x.dtype),
        in_specs=[pl.BlockSpec(memory_space=pltpu.VMEM)],
        out_specs=pl.BlockSpec(memory_space=pltpu.VMEM),
        scratch_shapes=[
            pltpu.SemaphoreType.DMA((chips,)),
            pltpu.SemaphoreType.DMA((chips,)),
            pltpu.SemaphoreType.DMA((chips,)),
            pltpu.SemaphoreType.DMA((chips,)),
            pltpu.SemaphoreType.DMA,
        ],
        compiler_params=pltpu.CompilerParams(
            collective_id=ident, has_side_effects=True, vmem_limit_bytes=32 << 20
        ),
    )(x)


def unpack(block, kt_ref, vt_ref, c_ref):
    lane = lax.broadcasted_iota(jnp.int32, (64, 128), 1)
    lane16 = lax.broadcasted_iota(jnp.int32, (16, 128), 1)
    for pair in range(2):
        first, second = block[2 * pair].astype(F32), block[2 * pair + 1].astype(F32)

        def rest(x):
            low = x[64:96]
            return jnp.concatenate([low, pltpu.roll(low, 64, 1)], axis=0)

        tails = jnp.where(lane < 64, rest(first), pltpu.roll(rest(second), 64, 1))
        tail16 = jnp.where(lane16 < 64, first[112:128], pltpu.roll(second[112:128], 64, 1))
        parts = [
            (first[0:64], first[96:112]),
            (tails, tail16),
            (second[0:64], second[96:112]),
        ]
        for tile, (p, c16) in enumerate(parts):
            cols = slice((3 * pair + tile) * 128, (3 * pair + tile + 1) * 128)
            scales = c16[0:8] + c16[8:16]
            c_ref[:, cols] = scales
            pb = p.astype(BF)
            kt_ref[0:64, cols] = pb
            kt_ref[128:192, cols] = pb
            s_row = scales[6:7]
            vt_ref[0:64, cols] = (p * s_row).astype(BF)
            s_hi = c16[6:7]
            s_lo = c16[14:15]
            row = lax.broadcasted_iota(jnp.int32, (16, 128), 0)
            extra = jnp.where(row == 0, s_hi, jnp.where(row == 1, s_lo, jnp.where(row == 2, 1.0, 0.0)))
            vt_ref[64:80, cols] = extra.astype(BF)


NT = (((1,), (1,)), ((), ()))


def attend_kernel(heads, rows, steps, g_ref, q_ref, bound_ref, qhat_ref, kh_ref, vh_ref, hbias_ref, aop_ref,
                  out_ref, kt, vt, cs, acc, m_ref, flag):
    hist_scale = LOG2E / math.sqrt(128.0)
    biggest = jnp.max(bound_ref[...])

    one_row = lax.broadcasted_iota(jnp.int32, (64, kt.shape[1]), 0)
    ones = jnp.where(one_row == 0, 1.0, 0.0).astype(BF)
    kt[64:128, :] = ones
    kt[192:256, :] = ones
    vt[80:128, :] = jnp.zeros((48, vt.shape[1]), BF)
    acc[...] = jnp.zeros_like(acc)
    m_ref[...] = bound_ref[...] - SPAN

    def hist_scores(h):
        s = lax.dot_general(qhat_ref[:, h * 128:(h + 1) * 128], kh_ref[:, h * 128:(h + 1) * 128], NT,
                            preferred_element_type=F32)
        return s * hist_scale + hbias_ref[0:1, :]

    @pl.when(biggest > SAFE)
    def _():
        for h in range(heads):
            sl = slice(h * rows, (h + 1) * rows)
            m_ref[sl, :] = jnp.broadcast_to(jnp.max(hist_scores(h), axis=1, keepdims=True), (rows, 128))

        @pl.loop(0, steps)
        def _(i):
            unpack([g_ref[4 * i + b] for b in range(4)], kt, vt, cs)
            for h in range(heads):
                sl = slice(h * rows, (h + 1) * rows)
                s = jnp.dot(q_ref[sl, :], kt[...], preferred_element_type=F32) * cs[h:h + 1, :]
                m_ref[sl, :] = jnp.maximum(m_ref[sl, :], jnp.max(s, axis=1, keepdims=True))

    @pl.loop(0, steps)
    def _(i):
        unpack([g_ref[4 * i + b] for b in range(4)], kt, vt, cs)

        def scores(h):
            return jnp.dot(q_ref[h * rows:(h + 1) * rows, :], kt[...], preferred_element_type=F32)

        ahead = scores(0)
        for h in range(heads):
            s = ahead
            if h + 1 < heads:
                ahead = scores(h + 1)
            sl = slice(h * rows, (h + 1) * rows)
            w = jnp.exp2(s * cs[h:h + 1, :] - m_ref[sl, 0:1]).astype(BF)
            acc[sl, :] += lax.dot_general(w, vt[...], NT, preferred_element_type=F32)

    for h in range(heads):
        sl = slice(h * rows, (h + 1) * rows)
        w = jnp.exp2(hist_scores(h) - m_ref[sl, 0:1])
        total = jnp.sum(w, axis=1, keepdims=True)
        o = jnp.dot(w.astype(BF), vh_ref[:, h * 128:(h + 1) * 128], preferred_element_type=F32)
        a = acc[sl, :]
        hi = a.astype(BF)
        lo = (a - hi.astype(F32)).astype(BF)
        o = o + jnp.dot(hi, aop_ref[0, :, h * 128:(h + 1) * 128], preferred_element_type=F32)
        o = o + jnp.dot(lo, aop_ref[0, :, h * 128:(h + 1) * 128], preferred_element_type=F32)
        o = o + jnp.dot(hi, aop_ref[1, :, h * 128:(h + 1) * 128], preferred_element_type=F32)
        total = total + a[:, 66:67]
        out_ref[:, h * 128:(h + 1) * 128] = (o / total).astype(BF)


def attend(gathered, qop, bound, qhat, kh, vh, hbias, aop):
    count = gathered.shape[0]
    heads = aop.shape[2] // 128
    rows = qhat.shape[0]
    vm = pl.BlockSpec(memory_space=pltpu.VMEM)
    return pl.pallas_call(
        functools.partial(attend_kernel, heads, rows, count // 4),
        out_shape=jax.ShapeDtypeStruct((rows, heads * 128), BF),
        in_specs=[vm] * 8,
        out_specs=vm,
        scratch_shapes=[
            pltpu.VMEM((256, 768), BF),
            pltpu.VMEM((128, 768), BF),
            pltpu.VMEM((8, 768), F32),
            pltpu.VMEM((heads * rows, 128), F32),
            pltpu.VMEM((heads * rows, 128), F32),
            pltpu.SMEM((1,), F32),
        ],
        compiler_params=pltpu.CompilerParams(vmem_limit_bytes=40 << 20),
    )(gathered, qop, bound, qhat, kh, vh, hbias, aop)


def low_rank_kernel(w_in_ref, gain_ref, embed_ref, hx_ref, wh_ref, gain_all_ref, wk_ref, wv_ref, kg_ref,
                    akc_ref, akg_ref, av_ref, kh_ref, vh_ref, pre, tok, acc_k, acc_v):
    step = pl.program_id(0)
    last = pl.num_programs(0) - 1
    width = pre.shape[1]
    chunk = w_in_ref.shape[1]
    slots = hx_ref.shape[0]

    @pl.when(step == 0)
    def _():
        square = jnp.zeros((slots, 1), F32)
        for j in range(width // chunk):
            cols = slice(j * chunk, (j + 1) * chunk)
            part = jnp.dot(hx_ref[...], wh_ref[:, cols], preferred_element_type=F32)
            pre[:, cols] = part
            square = square + jnp.sum(part * part, axis=1, keepdims=True)
        r = lax.rsqrt(square * (1.0 / width) + EPSILON)
        for j in range(width // chunk):
            cols = slice(j * chunk, (j + 1) * chunk)
            tok[j] = (pre[:, cols] * r * gain_all_ref[:, cols]).astype(BF)
        acc_k[...] = jnp.zeros_like(acc_k)
        acc_v[...] = jnp.zeros_like(acc_v)

    low = w_in_ref[...].astype(F32) * gain_ref[...]
    e = jnp.broadcast_to(embed_ref[...] * gain_ref[...], (16, chunk))
    low_hi = low.astype(BF)
    low_lo = (low - low_hi.astype(F32)).astype(BF)
    e_hi = e.astype(BF)
    e_lo = (e - e_hi.astype(F32)).astype(BF)
    left = jnp.concatenate([low_hi, low_lo, e_hi, e_lo, tok[step]], axis=0)
    acc_k[...] += jnp.dot(left, wk_ref[...], preferred_element_type=F32)
    acc_v[...] += jnp.dot(left, wv_ref[...], preferred_element_type=F32)

    @pl.when(step == last)
    def _():
        def parts(acc):
            a = acc[0:64, :] + acc[64:128, :]
            b = acc[128:144, :] + acc[144:160, :]
            row = lax.broadcasted_iota(jnp.int32, b.shape, 0)
            return a, b, row

        def put(ref, a, b, scale):
            full = jnp.concatenate([a, b, jnp.zeros((48, a.shape[1]), F32)], axis=0) * scale
            hi = full.astype(BF)
            ref[0] = hi
            ref[1] = (full - hi.astype(F32)).astype(BF)

        a, b, row = parts(acc_k)
        b = jnp.where(row == 0, b, 0.0)
        put(akc_ref, a, b, 1.0)
        put(akg_ref, a, b, kg_ref[...])
        a, b, row = parts(acc_v)
        put(av_ref, a, jnp.where(row < 2, b, 0.0), 1.0)
        for h in range(kh_ref.shape[1] // 128):
            cols = slice(h * 128, (h + 1) * 128)
            k = acc_k[160:, cols]
            r = lax.rsqrt(jnp.mean(k * k, axis=1, keepdims=True) + EPSILON)
            kh_ref[:, cols] = (k * r * kg_ref[:, cols]).astype(BF)
        vh_ref[...] = acc_v[160:, :].astype(BF)


def low_rank(w_in, gain, embed, hx, w_hist, w_key, w_value, kg):
    width = w_in.shape[1]
    cols = w_key.shape[1]
    slots = hx.shape[0]
    steps = 6
    chunk = width // steps
    whole = lambda shape: pl.BlockSpec(shape, lambda i: (0,) * len(shape))
    ops = jax.ShapeDtypeStruct((2, 128, cols), BF)
    kv = jax.ShapeDtypeStruct((slots, cols), BF)
    return pl.pallas_call(
        low_rank_kernel,
        out_shape=(ops, ops, ops, kv, kv),
        grid=(steps,),
        in_specs=[
            pl.BlockSpec((64, chunk), lambda i: (0, i)),
            pl.BlockSpec((1, chunk), lambda i: (0, i)),
            pl.BlockSpec((1, chunk), lambda i: (0, i)),
            whole(hx.shape), whole(w_hist.shape), whole((1, width)),
            pl.BlockSpec((chunk, cols), lambda i: (i, 0)),
            pl.BlockSpec((chunk, cols), lambda i: (i, 0)),
            whole((1, cols)),
        ],
        out_specs=(whole(ops.shape), whole(ops.shape), whole(ops.shape), whole(kv.shape), whole(kv.shape)),
        scratch_shapes=[
            pltpu.VMEM((slots, width), F32),
            pltpu.VMEM((steps, slots, chunk), BF),
            pltpu.VMEM((slots + 160, cols), F32),
            pltpu.VMEM((slots + 160, cols), F32),
        ],
        compiler_params=pltpu.CompilerParams(vmem_limit_bytes=48 << 20),
        cost_estimate=pl.CostEstimate(flops=4 * 672 * width * cols, bytes_accessed=12 << 20, transcendentals=0),
    )(w_in, gain, embed, hx, w_hist, gain, w_key, w_value, kg)


def encode_kernel(early_ref, feats_ref, cw_ref, bias_ref, lw_ref, noise_ref, sigma_ref, out_ref):
    grp = lax.axis_index("grp")
    sigma = sigma_ref[0]
    frames, channels, pixels = feats_ref.shape
    window = [early_ref[0], early_ref[1], feats_ref[0], feats_ref[1]]
    pixel = lax.broadcasted_iota(jnp.int32, (pixels, out_ref.shape[1]), 0)
    col = lax.broadcasted_iota(jnp.int32, (pixels, out_ref.shape[1]), 1)
    rows = [jnp.zeros((lw_ref.shape[0], out_ref.shape[1]), F32) for _ in range(4)]
    for t in range(frames):
        total = jnp.zeros((channels, pixels), F32)
        for tap in range(3):
            total = total + jnp.dot(cw_ref[tap], window[2 + t - tap], preferred_element_type=F32)
        total = total + bias_ref[...]
        hidden = (total * (1.0 / (1.0 + jnp.exp(-total)))).astype(BF)
        latent = jnp.dot(lw_ref[...], hidden, preferred_element_type=F32)
        noisy = ((1.0 - sigma) * latent + sigma * noise_ref[t].astype(F32)).astype(BF)
        for i in range(4):
            hit = (pixel % 4 == i) & (col == t * (pixels // 2) + grp * (pixels // 4) + pixel // 4)
            rows[i] = rows[i] + jnp.dot(noisy, jnp.where(hit, 1.0, 0.0).astype(BF), preferred_element_type=F32)
    out_ref[...] = jnp.concatenate(rows, axis=0).astype(BF)


def encode(early, feats, conv_weight, conv_bias, lat_weight, noise, sigma):
    vm = pl.BlockSpec(memory_space=pltpu.VMEM)
    return pl.pallas_call(
        encode_kernel,
        out_shape=jax.ShapeDtypeStruct((4 * lat_weight.shape[0], 256), BF),
        in_specs=[vm] * 6 + [pl.BlockSpec(memory_space=pltpu.SMEM)],
        out_specs=vm,
    )(early, feats, conv_weight, conv_bias, lat_weight, noise, sigma)


def tokens_kernel(mine_ref, other_ref, w_in_ref, embed_ref, gain_ref, akc_ref, tok_ref, pay_ref, x_ref):
    rows, width = tok_ref.shape
    heads = akc_ref.shape[2] // 128
    chunk = 512
    pt = mine_ref[...].astype(F32) + other_ref[...].astype(F32)
    lanes = pt.shape[1]
    row = lax.broadcasted_iota(jnp.int32, (64, lanes), 0)
    tall = jnp.concatenate([pt, jnp.where(row == 0, 1.0, 0.0)], axis=0)
    px = jnp.transpose(tall)[:rows].astype(BF)
    p = px[:, :64]
    square = jnp.zeros((rows, 1), F32)
    square_row = jnp.zeros((8, rows), F32)
    ones = jnp.ones((8, chunk), BF)
    for j in range(width // chunk):
        cols = slice(j * chunk, (j + 1) * chunk)
        x = jnp.dot(p, w_in_ref[:, cols], preferred_element_type=F32) + embed_ref[:, cols]
        x_ref[:, cols] = x
        x2 = x * x
        square = square + jnp.sum(x2, axis=1, keepdims=True)
        hi, lo = split(x2)
        square_row = square_row + lax.dot_general(ones, hi, NT, preferred_element_type=F32)
        square_row = square_row + lax.dot_general(ones, lo, NT, preferred_element_type=F32)
    s = lax.rsqrt(square * (1.0 / width) + EPSILON)
    for j in range(width // chunk):
        cols = slice(j * chunk, (j + 1) * chunk)
        tok_ref[:, cols] = (x_ref[:, cols] * s * gain_ref[:, cols]).astype(BF)
    s_row = lax.rsqrt(square_row * (1.0 / width) + EPSILON)
    y = jnp.dot(px, akc_ref[0], preferred_element_type=F32) + jnp.dot(px, akc_ref[1], preferred_element_type=F32)
    hi, lo = split(y * y)
    r8 = lax.broadcasted_iota(jnp.int32, (8, heads * 128), 0)
    c8 = lax.broadcasted_iota(jnp.int32, (8, heads * 128), 1)
    pick = jnp.where(c8 // 128 == r8, 1.0, 0.0).astype(BF)
    mean = (lax.dot_general(pick, hi, NT, preferred_element_type=F32)
            + lax.dot_general(pick, lo, NT, preferred_element_type=F32)) * (1.0 / 128)
    c = s_row * lax.rsqrt(s_row * s_row * mean + EPSILON) * (LOG2E / math.sqrt(128.0))
    r = lax.broadcasted_iota(jnp.int32, (8, rows), 0)
    both = jnp.where(r < heads, c, jnp.where(r == 6, s_row, 0.0))
    both = jnp.concatenate([both, jnp.zeros((8, 256 - rows), F32)], axis=1)
    hi8 = both.astype(BF).astype(F32)
    c16 = jnp.concatenate([hi8, both - hi8], axis=0)
    pay_ref[0:64, :] = pt[:, 0:128].astype(BF)
    lane = lax.broadcasted_iota(jnp.int32, (32, 128), 1)
    pay_ref[64:96, :] = jnp.where(lane < 64, pt[0:32, 128:256], pltpu.roll(pt[32:64, 128:256], 64, 1)).astype(BF)
    pay_ref[96:112, :] = c16[:, 0:128].astype(BF)
    pay_ref[112:128, :] = c16[:, 128:256].astype(BF)


def make_tokens(mine, other, w_in, embed, gain, akc, rows):
    vm = pl.BlockSpec(memory_space=pltpu.VMEM)
    width = w_in.shape[1]
    return pl.pallas_call(
        tokens_kernel,
        out_shape=(jax.ShapeDtypeStruct((rows, width), BF), jax.ShapeDtypeStruct((128, 128), BF)),
        in_specs=[vm] * 6,
        out_specs=(vm, vm),
        scratch_shapes=[pltpu.VMEM((rows, width), F32)],
        compiler_params=pltpu.CompilerParams(vmem_limit_bytes=24 << 20),
    )(mine, other, w_in, embed, gain, akc)


def query_kernel(tok_ref, wq_ref, qg_ref, kg_ref, akg_ref, qhat_ref, qop_ref, bound_ref):
    q = jnp.dot(tok_ref[...], wq_ref[...], preferred_element_type=F32)
    q = q * lax.rsqrt(jnp.mean(q * q, axis=1, keepdims=True) + EPSILON) * qg_ref[...]
    qb = q.astype(BF)
    qhat_ref[...] = qb
    qp = (lax.dot_general(qb, akg_ref[0], NT, preferred_element_type=F32)
          + lax.dot_general(qb, akg_ref[1], NT, preferred_element_type=F32))
    hi, lo = split(qp)
    qop_ref[:, 0:128] = hi
    qop_ref[:, 128:256] = lo
    reach = qb.astype(F32) * kg_ref[...]
    size = jnp.sqrt(jnp.sum(reach * reach, axis=1, keepdims=True)) * (LOG2E * 1.01)
    bound_ref[...] = jnp.broadcast_to(size, bound_ref.shape)


def make_query(tokens, w_query, q_gain, k_gain, akg):
    rows, width = tokens.shape
    heads = w_query.shape[1] // 128
    return pl.pallas_call(
        query_kernel,
        out_shape=(jax.ShapeDtypeStruct((rows, heads * 128), BF), jax.ShapeDtypeStruct((heads * rows, 256), BF),
                   jax.ShapeDtypeStruct((heads * rows, 128), F32)),
        grid=(heads,),
        in_specs=[
            pl.BlockSpec((rows, width), lambda h: (0, 0)),
            pl.BlockSpec((width, 128), lambda h: (0, h)),
            pl.BlockSpec((1, 128), lambda h: (0, 0)),
            pl.BlockSpec((1, 128), lambda h: (0, 0)),
            pl.BlockSpec((2, 128, 128), lambda h: (0, 0, h)),
        ],
        out_specs=(pl.BlockSpec((rows, 128), lambda h: (0, h)), pl.BlockSpec((rows, 256), lambda h: (h, 0)),
                   pl.BlockSpec((rows, 128), lambda h: (h, 0))),
        compiler_params=pltpu.CompilerParams(vmem_limit_bytes=24 << 20),
    )(tokens, w_query, q_gain, k_gain, akg)


def local(
    feats, conv_weight, conv_bias, latent_projection_weight, noise, step_index, hist, hist_level, hist_count,
    w_in, w_hist, norm_gain, w_query, w_key, w_value, q_gain, k_gain, w_out,
):
    grp = lax.axis_index("grp")
    seq_count = lax.axis_size("seq")
    frames, channels, pixels = feats.shape
    width = w_in.shape[1]
    head_size = q_gain.shape[0]
    heads = w_query.shape[1] // head_size
    half = w_out.shape[1] // 2
    rows = frames * pixels // 2

    earlier = lax.ppermute(feats, "seq", [(i, i + 1) for i in range(seq_count - 1)])

    spread = [jnp.where((hist_level == l)[:, None], hist, jnp.zeros_like(hist)) for l in range(3)]
    spread = jnp.concatenate([jnp.concatenate(spread[:2], axis=1), jnp.pad(spread[2], ((0, 0), (0, 64)))], axis=0)
    spread = gather_blocks(spread, seq_count, 1)
    slots = hist.shape[0]
    hx = jnp.concatenate([spread[:, :slots], spread[:, slots:, :64]], axis=2).reshape(seq_count * slots, 192)

    embed = time_embed(step_index, width)[None]
    gain = norm_gain[None]
    w_in = w_in.reshape(-1, 4, width).transpose(1, 0, 2).reshape(-1, width)
    kg = jnp.tile(k_gain, heads)[None]
    akc, akg, av, k_hist, v_hist = low_rank(w_in, gain, embed, hx, w_hist.reshape(-1, width), w_key, w_value, kg)

    sigma = (STEPS - step_index.astype(F32)) / STEPS
    mine = encode(earlier, feats, conv_weight, conv_bias[:, None], latent_projection_weight, noise, sigma)
    other = swap(mine)
    tokens, payload = make_tokens(mine, other, w_in, embed, gain, akc, rows)
    qhat, qop, bound = make_query(tokens, w_query, q_gain[None], k_gain[None], akg)
    gathered = gather_blocks(payload, seq_count, 0)

    live = jnp.arange(slots, dtype=jnp.int32)[None, :] < hist_count[:, None]
    hbias = jnp.broadcast_to(jnp.where(live, 0.0, -1e30).reshape(1, -1), (8, seq_count * slots)).astype(F32)

    w_far = swap(lax.dynamic_slice_in_dim(w_out, (1 - grp) * half, half, 1))
    w_near = lax.dynamic_slice_in_dim(w_out, grp * half, half, 1)

    heads_out = attend(gathered, qop, bound, qhat, k_hist, v_hist, hbias, av)
    heads_far = swap(heads_out)
    out = jnp.dot(heads_out, w_near, preferred_element_type=F32) + jnp.dot(heads_far, w_far, preferred_element_type=F32)
    return out.astype(BF)


def solution(mesh):
    placed = (
        P("seq", None, "grp"), P(), P(), P(), P("seq", None, "grp"), P(), P("seq", None), P("seq"), P(), P(), P(), P(),
        P(None, "grp"), P(None, "grp"), P(None, "grp"), P(), P(), P("grp", None),
    )
    return jax.shard_map(local, mesh=mesh, in_specs=placed, out_specs=P("seq", "grp"), check_vma=False)
```

time: 370 us -> 174 us (0.47)
  waiting for transfers between devices: 191 us -> 11.3 us
  Pallas kernels: 0 us -> 140 us
  matrix products: 78.9 us -> 5.42 us
  local copies, waits for them, and re-layouts: 55.3 us -> 9.61 us
  other arithmetic: 25 us -> 0.35 us
  between operations: 14 us -> 0.93 us
    all_gather x3 -> x0, waiting for transfers between devices: 164 us -> none  [the longest x1 96.6 us: local(): key_piece = lax.all_gather(flattened_keys, 'seq', axis=0, tiled=True)]
    pallas_call x0 -> x7, Pallas kernels: none -> 140 us  [the longest x2 80.8 us: gather_blocks(): pl.pallas_call(functools.partial(gather_kernel, chips), out_shape=jax.Sha...]
    dot_general x13 -> x2, matrix products: 78.9 us -> 5.42 us  [the longest x1 3.14 us: local(): jnp.dot(heads_out, w_near, preferred_element_type=F32)]
    all_gather x2 -> x0, local copies, waits for them, and re-layouts: 47.6 us -> none  [the longest x1 23.8 us: local(): key_piece = lax.all_gather(flattened_keys, 'seq', axis=0, tiled=True)]
    reduce_scatter x1 -> x0, waiting for transfers between devices: 24.3 us -> none  [local(): lax.psum_scatter(partial_out.astype(jnp.bfloat16), 'grp', scatter_dimensi...]
    reduce_sum x3 -> x0, other arithmetic: 22.3 us -> none  [the longest x1 21.4 us: local(): new_sum = jnp.sum(soft, axis=-1)]
    ppermute x1 -> x4, waiting for transfers between devices: 3.01 us -> 11.3 us  [the longest x3 11.3 us: swap(): return lax.ppermute(value, 'grp', [(0, 1), (1, 0)])]
  transfers between devices with their start and end apart: 5 -> 4, of which waited for: 5 -> 2; matrix products, arithmetic and copies ran while one was open for 26% -> 1% of each run, Pallas kernels for 0% -> 81%
where the time goes in v1:
time: 174 us; the launch traced here: 173 us
  Pallas kernels  140 us (80%)
  waiting for transfers between devices  11.3 us (6%)
  local copies, waits for them, and re-layouts  9.61 us (6%)
  matrix products  5.42 us (3%)
  starting transfers between devices  5.16 us (3%)
    pallas_call x2, Pallas kernels, gather_blocks(): pl.pallas_call(functools.partial(gather_kernel, chips), out_shape=jax.Sha...  80.8 us
    pallas_call x1, Pallas kernels, attend(): pl.pallas_call(functools.partial(attend_kernel, heads, rows, count // 4),...  37.4 us
    pallas_call x1, Pallas kernels, low_rank(): pl.pallas_call(low_rank_kernel, out_shape=(ops, ops, ops, kv, kv), grid=(...  11.7 us
    ppermute x3, waiting for transfers between devices, swap(): return lax.ppermute(value, 'grp', [(0, 1), (1, 0)])  11.3 us
    unnamed x31, local copies, waits for them, and re-layouts  5.17 us
    pallas_call x1, Pallas kernels, make_query(): pl.pallas_call(query_kernel, out_shape=(jax.ShapeDtypeStruct((rows, heads...  5.03 us
  transfers between devices with their start and end apart: 4, of which 2 were waited for; matrix products, arithmetic and copies ran while one was open for 1% of the time, Pallas kernels for 81%

profile of v1, /device:TPU:4, one launch (start us, length us, event | category | flops | bytes accessed | tf_op | source)
XLA Modules:
  0.0 172.6 jit_solution(9077719445733370735)
XLA Ops:
  0.0 3.3 %constant_dynamic-slice_fusion = bf16[768,1536]{1,0:T(8,128)(2,1)} fusion(bf16[768,3072]{1,0:T(8,128)(2,1)} %param.35, s32[]{:T(128)S(6)} %select_n.33), kind=kLoop, calls=%fused_computation.18 | loop fusion | bytes 4718596 | tf_op jit(solution)/shard_map/dynamic_slice | solution.py:496
  3.3 1.2 collective-permute-start.3
  4.5 0.1 copy.23.feats_ref
  4.7 1.9 %collective-permute-start = (bf16[2,128,192]{2,1,0:T(8,128)(2,1)S(1)}, bf16[2,128,192]{2,1,0:T(8,128)(2,1)S(1)}, u32[]{:S(2)}, u32[]{:S(2)}) collective-permute-start(bf16[2,128,192]{2,1,0:T(8,128)(2,1)S(1)} %copy.23.feats_ref), channel_id=1, source_target_pairs={{0,1},{1,2},{2,3},{3,4},{4,5},{5,6},{6,7},{7,8},{8,9},{9,10},{10,1... | collective-permute-start | bytes 294920 | tf_op jit(solution)/shard_map/ppermute | solution.py:472
  6.6 0.1 broadcast_select_fusion.2
  6.7 0.1 fusion.6.x_ref
  6.8 59.9 %shard_map.173 = bf16[64,16,128]{2,1,0:T(8,128)(2,1)S(1)} custom-call(bf16[16,128]{1,0:T(8,128)(2,1)S(1)} %fusion.6.x_ref), custom_call_target="tpu_custom_call" | custom-call | tf_op jit(solution)/shard_map/pallas_call | solution.py:97
  67.4 0.1 reshape.37
  67.5 0.1 copy.26
  67.7 0.1 fusion.3
  67.8 0.0 copy-start.5
  67.8 1.3 copy-done.5
  69.1 11.7 %shard_map.174 = (bf16[2,128,768]{2,1,0:T(8,128)(2,1)S(1)}, bf16[2,128,768]{2,1,0:T(8,128)(2,1)S(1)}, bf16[2,128,768]{2,1,0:T(8,128)(2,1)S(1)}, bf16[512,768]{1,0:T(8,128)(2,1)S(1)}, bf16[512,768]{1,0:T(8,128)(2,1)S(1)}) custom-call(bf16[64,3072]{1,0:T(8,128)(2,1)S(1)} %bitcast.21, f32[1,3072]{1,0:T(1,128)S(1)} %bitcast.25, f32[1,3072]{1,0:T(1,128)S(1)} %bitcast.23, ...), custom_call_target="tpu_custom_call" | custom-call | flops 6341787648 | bytes 12582912 | tf_op jit(solution)/shard_map/pallas_call | solution.py:306
  80.9 0.0 copy-start.4
  80.9 0.7 copy.25.bias_ref
  81.6 0.7 copy-done.8
  82.3 2.5 %shard_map.172.mine_ref = bf16[64,256]{1,0:T(8,128)(2,1)} custom-call(bf16[2,128,192]{2,1,0:T(8,128)(2,1)} %copy-done.8, bf16[2,128,192]{2,1,0:T(8,128)(2,1)} %copy-done.6, bf16[3,128,128]{2,1,0:T(8,128)(2,1)} %cw_ref.1, f32[128,1]{1,0:T(8,128)} %copy.25.bias_ref, bf16[16,128]{1,0:T(8,128)(2,1)} %lw_ref.1, bf16[2,16,192]{2,1,0:T(8,128)(2,1)} %noise_ref.1, ...), custom_call_target="tpu_custom_call" | custom-call | tf_op jit(solution)/shard_map/pallas_call | solution.py:355
  84.8 1.1 collective-permute-start.1
  85.9 0.1 fusion.2
  86.0 0.1 select_n.31
  86.1 2.8 %collective-permute-done.1.other_ref = bf16[64,256]{1,0:T(8,128)(2,1)S(1)} collective-permute-done((bf16[64,256]{1,0:T(8,128)(2,1)}, bf16[64,256]{1,0:T(8,128)(2,1)S(1)}, u32[]{:S(2)}, u32[]{:S(2)}) %collective-permute-start.1) | collective-permute-done | bytes 32800 | tf_op jit(solution)/shard_map/ppermute | solution.py:39
  88.9 0.8 copy-done.1
  89.6 2.3 %shard_map.175 = (bf16[192,3072]{1,0:T(8,128)(2,1)S(1)}, bf16[128,128]{1,0:T(8,128)(2,1)S(1)}) custom-call(bf16[64,256]{1,0:T(8,128)(2,1)S(1)} %copy-done.1, bf16[64,256]{1,0:T(8,128)(2,1)S(1)} %collective-permute-done.1.other_ref, bf16[64,3072]{1,0:T(8,128)(2,1)S(1)} %bitcast.22, f32[1,3072]{1,0:T(1,128)S(1)} %bitcast.24, f32[1,3072]{1,0:T(1,128)S(1)} %bitcast.27, ...), custom_call_target="tpu_custom_call" | custom-call | tf_op jit(solution)/shard_map/pallas_call | solution.py:413
  92.0 21.0 %shard_map.176.g_ref = bf16[64,128,128]{2,1,0:T(8,128)(2,1)S(1)} custom-call(bf16[128,128]{1,0:T(8,128)(2,1)S(1)} %get-tuple-element.16.x_ref), custom_call_target="tpu_custom_call" | custom-call | tf_op jit(solution)/shard_map/pallas_call | solution.py:97
  112.9 0.0 copy-start
  113.0 2.3 %copy-done = bf16[3072,768]{1,0:T(8,128)(2,1)S(1)} copy-done((bf16[3072,768]{1,0:T(8,128)(2,1)S(1)}, bf16[3072,768]{1,0:T(8,128)(2,1)}, u32[]{:S(2)}) %copy-start) | copy-done | bytes 4718616
  115.3 5.0 %shard_map.177 = (bf16[192,768]{1,0:T(8,128)(2,1)S(1)}, bf16[1152,256]{1,0:T(8,128)(2,1)S(1)}, f32[1152,128]{1,0:T(8,128)S(1)}) custom-call(bf16[192,3072]{1,0:T(8,128)(2,1)S(1)} %get-tuple-element.17.tok_ref, bf16[3072,768]{1,0:T(8,128)(2,1)S(1)} %copy-done, f32[1,128]{1,0:T(1,128)S(1)} %bitcast.30, f32[1,128]{1,0:T(1,128)S(1)} %bitcast.29, ...), custom_call_target="tpu_custom_call" | custom-call | tf_op jit(solution)/shard_map/pallas_call | solution.py:441
  120.3 37.4 %shard_map.178 = bf16[192,768]{1,0:T(8,128)(2,1)S(1)} custom-call(bf16[64,128,128]{2,1,0:T(8,128)(2,1)S(1)} %shard_map.176.g_ref, bf16[1152,256]{1,0:T(8,128)(2,1)S(1)} %get-tuple-element.19.q_ref, f32[1152,128]{1,0:T(8,128)S(1)} %get-tuple-element.20.bound_ref, bf16[192,768]{1,0:T(8,128)(2,1)S(1)} %get-tuple-element.21.qhat_ref, ...), custom_call_target="tpu_custom_call" | custom-call | tf_op jit(solution)/shard_map/pallas_call | solution.py:219
  157.8 0.9 collective-permute-start.2
  158.7 8.5 %collective-permute-done.2 = bf16[192,768]{1,0:T(8,128)(2,1)S(1)} collective-permute-done((bf16[192,768]{1,0:T(8,128)(2,1)S(1)}, bf16[192,768]{1,0:T(8,128)(2,1)S(1)}, u32[]{:S(2)}, u32[]{:S(2)}) %collective-permute-start.2) | collective-permute-done | bytes 294944 | tf_op jit(solution)/shard_map/ppermute | solution.py:39
  167.1 2.3 %fusion.8 = f32[192,1536]{1,0:T(8,128)S(1)} fusion(bf16[192,768]{1,0:T(8,128)(2,1)S(1)} %collective-permute-done.2, bf16[768,1536]{1,0:T(8,128)(2,1)} %collective-permute-done.3), kind=kOutput, calls=%fused_computation.23 | convolution fusion | flops 452984832 | bytes 3833856 | tf_op jit(solution)/shard_map/dot_general | solution.py:501
  169.4 3.1 %fusion = bf16[192,1536]{1,0:T(8,128)(2,1)} fusion(f32[192,1536]{1,0:T(8,128)S(1)} %fusion.8, bf16[192,768]{1,0:T(8,128)(2,1)S(1)} %shard_map.178, bf16[768,3072]{1,0:T(8,128)(2,1)} %param.35, s32[]{:T(128)S(6)} %select_n.32), kind=kOutput, calls=%fused_computation.1 | convolution fusion | flops 453574656 | bytes 4423684 | tf_op jit(solution)/shard_map/dot_general | solution.py:501
  (31 shorter events, 0.1 us)
Async XLA Ops:
  0.0 4.5 %copy-start.9 = (bf16[2,128,192]{1,2,0:T(8,128)(2,1)S(1)}, bf16[2,128,192]{1,2,0:T(8,128)(2,1)}, u32[]{:S(2)}) copy-start(bf16[2,128,192]{1,2,0:T(8,128)(2,1)} %param.18) | copy-start | bytes 294916
  0.0 6.6 %copy-start.13 = (s32[8]{0:T(128)S(1)}, s32[8]{0:T(128)}, u32[]{:S(2)}) copy-start(s32[8]{0:T(128)} %param.25) | copy-start | bytes 100
  0.0 6.6 %copy-start.10 = (bf16[8,64]{1,0:T(8,128)(2,1)S(1)}, bf16[8,64]{1,0:T(8,128)(2,1)}, u32[]{:S(2)}) copy-start(bf16[8,64]{1,0:T(8,128)(2,1)} %param.24) | copy-start | bytes 3076
  0.0 67.3 %copy-start.7 = (bf16[64,3072]{1,0:T(8,128)(2,1)S(1)}, bf16[64,3072]{1,0:T(8,128)(2,1)}, u32[]{:S(2)}) copy-start(bf16[64,3072]{1,0:T(8,128)(2,1)} %param.27) | copy-start | bytes 1179652
  3.3 64.3 %copy-start.3 = (f32[128]{0:T(128)S(1)}, f32[128]{0:T(128)}, u32[]{:S(2)}) copy-start(f32[128]{0:T(128)} %param.34) | copy-start | bytes 1540
  3.3 64.5 %copy-start.2 = (f32[3072]{0:T(1024)S(1)}, f32[3072]{0:T(1024)}, u32[]{:S(2)}) copy-start(f32[3072]{0:T(1024)} %param.29) | copy-start | bytes 36868
  3.3 163.8 %collective-permute-start.3 = (bf16[768,1536]{1,0:T(8,128)(2,1)}, bf16[768,1536]{1,0:T(8,128)(2,1)}, u32[]{:S(2)}, u32[]{:S(2)}) collective-permute-start(bf16[768,1536]{1,0:T(8,128)(2,1)} %constant_dynamic-slice_fusion), channel_id=1, source_target_pairs={{0,64},{64,0},{1,65},{65,1},{2,66},{66,2},{3,67},{67,3},{4,68},{68... | collective-permute-start | bytes 7077896 | tf_op jit(solution)/shard_map/ppermute | solution.py:39
  4.7 76.2 %copy-start.6 = (bf16[2,128,192]{2,1,0:T(8,128)(2,1)}, bf16[2,128,192]{2,1,0:T(8,128)(2,1)S(1)}, u32[]{:S(2)}) copy-start(bf16[2,128,192]{2,1,0:T(8,128)(2,1)S(1)} %copy.23.feats_ref) | copy-start | bytes 294916
  4.7 77.0 %collective-permute-start = (bf16[2,128,192]{2,1,0:T(8,128)(2,1)S(1)}, bf16[2,128,192]{2,1,0:T(8,128)(2,1)S(1)}, u32[]{:S(2)}, u32[]{:S(2)}) collective-permute-start(bf16[2,128,192]{2,1,0:T(8,128)(2,1)S(1)} %copy.23.feats_ref), channel_id=1, source_target_pairs={{0,1},{1,2},{2,3},{3,4},{4,5},{5,6},{6,7},{7,8},{8,9},{9,10},{10,1... | collective-permute-start | bytes 294920 | tf_op jit(solution)/shard_map/ppermute | solution.py:472
  67.8 1.3 copy-start.5
  69.1 11.8 %copy-start.11 = (f32[128]{0:T(128)S(1)}, f32[128]{0:T(128)}, u32[]{:S(2)}) copy-start(f32[128]{0:T(128)} %param.20) | copy-start | bytes 1540
  69.1 16.8 %copy-start.12 = (s32[64]{0:T(128)S(1)}, s32[64]{0:T(128)}, u32[]{:S(2)}) copy-start(s32[64]{0:T(128)} %param.26) | copy-start | bytes 772
  80.9 32.1 %copy-start.4 = (f32[128]{0:T(128)S(1)}, f32[128]{0:T(128)}, u32[]{:S(2)}) copy-start(f32[128]{0:T(128)} %param.33) | copy-start | bytes 1540
  81.6 0.7 copy-start.8
  84.8 4.1 %collective-permute-start.1 = (bf16[64,256]{1,0:T(8,128)(2,1)}, bf16[64,256]{1,0:T(8,128)(2,1)S(1)}, u32[]{:S(2)}, u32[]{:S(2)}) collective-permute-start(bf16[64,256]{1,0:T(8,128)(2,1)} %shard_map.172.mine_ref), channel_id=1, source_target_pairs={{0,64},{64,0},{1,65},{65,1},{2,66},{66,2},{3,67},{67,3},{4,68},{68... | collective-permute-start | bytes 98312 | tf_op jit(solution)/shard_map/ppermute | solution.py:39
  88.9 0.8 copy-start.1
  112.9 2.3 %copy-start = (bf16[3072,768]{1,0:T(8,128)(2,1)S(1)}, bf16[3072,768]{1,0:T(8,128)(2,1)}, u32[]{:S(2)}) copy-start(bf16[3072,768]{1,0:T(8,128)(2,1)} %wq_ref.1) | copy-start | bytes 14155780
  157.8 9.4 %collective-permute-start.2 = (bf16[192,768]{1,0:T(8,128)(2,1)S(1)}, bf16[192,768]{1,0:T(8,128)(2,1)S(1)}, u32[]{:S(2)}, u32[]{:S(2)}) collective-permute-start(bf16[192,768]{1,0:T(8,128)(2,1)S(1)} %shard_map.178), channel_id=1, source_target_pairs={{0,64},{64,0},{1,65},{65,1},{2,66},{66,2},{3,67},{67,3},{4,68},{68... | collective-permute-start | bytes 884744 | tf_op jit(solution)/shard_map/ppermute | solution.py:39

commit v2 on v0

v2 whole, which is shorter than its diff:
```python
import functools
import math

import jax
import jax.numpy as jnp
from jax import lax
from jax.experimental import pallas as pl
from jax.experimental.pallas import tpu as pltpu
from jax.sharding import PartitionSpec as P

STEPS = 50
EPSILON = 1e-06
LOG2E = math.log2(math.e)
MESH = pl.DeviceIdType.MESH
BF = jnp.bfloat16
F32 = jnp.float32
LOW = -1e30


def split(x):
    hi = x.astype(BF)
    return hi, (x - hi.astype(F32)).astype(BF)


def unpack(block, kt_ref, vt_ref, c_ref):
    lane = lax.broadcasted_iota(jnp.int32, (64, 128), 1)
    lane16 = lax.broadcasted_iota(jnp.int32, (16, 128), 1)
    for pair in range(2):
        first, second = block[2 * pair].astype(F32), block[2 * pair + 1].astype(F32)

        def rest(x):
            low = x[64:96]
            return jnp.concatenate([low, pltpu.roll(low, 64, 1)], axis=0)

        tails = jnp.where(lane < 64, rest(first), pltpu.roll(rest(second), 64, 1))
        tail16 = jnp.where(lane16 < 64, first[112:128], pltpu.roll(second[112:128], 64, 1))
        parts = [
            (first[0:64], first[96:112]),
            (tails, tail16),
            (second[0:64], second[96:112]),
        ]
        for tile, (p, c16) in enumerate(parts):
            cols = slice((3 * pair + tile) * 128, (3 * pair + tile + 1) * 128)
            scales = c16[0:8] + c16[8:16]
            c_ref[:, cols] = scales
            pb = p.astype(BF)
            kt_ref[0:64, cols] = pb
            kt_ref[128:192, cols] = pb
            s_row = scales[6:7]
            vt_ref[0:64, cols] = (p * s_row).astype(BF)
            s_hi = c16[6:7]
            s_lo = c16[14:15]
            row = lax.broadcasted_iota(jnp.int32, (16, 128), 0)
            extra = jnp.where(row == 0, s_hi, jnp.where(row == 1, s_lo, jnp.where(row == 2, 1.0, 0.0)))
            vt_ref[64:80, cols] = extra.astype(BF)


NT = (((1,), (1,)), ((), ()))


def front_kernel(step_ref, level_ref, feats_ref, cw_ref, bias_ref, lw_ref, noise_ref, hist_ref, w_in_ref, wh_ref,
                 gain_ref, kg_ref, wk_hbm, wv_hbm, wout_hbm,
                 tok_ref, pay_ref, akg_ref, av_ref, akh_ref, avh_ref, far_ref,
                 early, wk, wv, acc_k, acc_v, x_ref, akc, w_perm, wave, mine, other,
                 wk_sem, wv_sem, send_sem, recv_sem):
    grp = lax.axis_index("grp")
    seq = lax.axis_index("seq")
    count = lax.axis_size("seq")
    core = seq % 2
    sibling = seq + 1 - 2 * core
    across = seq + 8 - 16 * ((seq // 8) % 2)
    after, before = (seq + 1) % count, (seq + count - 1) % count
    frames, channels, pixels = feats_ref.shape
    rows, width = tok_ref.shape
    cols = kg_ref.shape[1] * 6
    heads = cols // 128
    chunk = 512
    quarter = far_ref.shape[0] // 4
    half = far_ref.shape[1]

    loads = []
    for j in range(width // chunk):
        part = pl.ds(j * chunk, chunk)
        for source, into, sem in ((wk_hbm, wk, wk_sem), (wv_hbm, wv, wv_sem)):
            load = pltpu.make_async_copy(source.at[part], into.at[part], sem.at[j])
            load.start()
            loads.append(load)

    barrier = pltpu.get_barrier_semaphore()
    for there in ((1 - grp, seq), (1 - grp, across), (grp, sibling), (grp, after), (grp, before)):
        pl.semaphore_signal(barrier, inc=1, device_id=there, device_id_type=MESH)
    pl.semaphore_wait(barrier, 5)

    def send(n, source, into, there):
        return pltpu.make_async_remote_copy(
            src_ref=source, dst_ref=into, send_sem=send_sem.at[n], recv_sem=recv_sem.at[n],
            device_id=there, device_id_type=MESH)

    halo = send(0, feats_ref, early, (grp, after))
    halo.start()
    first_rows = pl.ds(pl.multiple_of(2 * core * quarter, quarter), quarter)
    second_rows = pl.ds(pl.multiple_of((2 * core + 1) * quarter, quarter), quarter)
    far_cols = pl.ds(pl.multiple_of((1 - grp) * half, half), half)
    piece_a = send(1, wout_hbm.at[first_rows, far_cols], far_ref.at[first_rows], (1 - grp, seq))
    piece_b = send(2, wout_hbm.at[second_rows, far_cols], far_ref.at[second_rows], (1 - grp, across))
    piece_a.start()
    piece_b.start()

    step = step_ref[0].astype(F32)
    place = lax.broadcasted_iota(jnp.int32, (8, width), 1)
    turn = jnp.where(place < width // 2, place, place - width // 2).astype(F32)
    angle = step * jnp.exp(turn * (-math.log(10000.0) / (width // 2)))
    wave[...] = jnp.where(place < width // 2, jnp.cos(angle), jnp.sin(angle))
    lane = lax.broadcasted_iota(jnp.int32, (16, 128), 1)
    line = lax.broadcasted_iota(jnp.int32, (16, 128), 0)
    level = jnp.zeros((16, 128), F32)
    for r in range(8):
        level = jnp.where(line == r, level_ref[r].astype(F32), level)
    base = jnp.concatenate([hist_ref[...].astype(F32), jnp.zeros((8, 64), F32)], axis=1)
    base = jnp.concatenate([base, jnp.zeros((8, 128), F32)], axis=0)
    moved = pltpu.roll(base, 64, 1)
    spread = jnp.concatenate([
        jnp.where(level == jnp.where(lane < 64, 0.0, 1.0), base + moved, 0.0),
        jnp.where(level == 2.0, base, 0.0)], axis=1).astype(BF)
    r64 = lax.broadcasted_iota(jnp.int32, (64, 64), 0)
    c64 = lax.broadcasted_iota(jnp.int32, (64, 64), 1)
    order = jnp.where(c64 == (r64 % 16) * 4 + r64 // 16, 1.0, 0.0).astype(BF)

    square = jnp.zeros((16, 1), F32)
    for j in range(width // chunk):
        part = slice(j * chunk, (j + 1) * chunk)
        gain = gain_ref[:, part]
        low = jnp.dot(order, w_in_ref[:, part], preferred_element_type=F32)
        w_perm[:, part] = low.astype(BF)
        low_hi, low_lo = split(low * gain)
        e_hi, e_lo = split(jnp.concatenate([wave[:, part]] * 2, axis=0) * gain)
        h = wh_ref[:, part]
        h_hi, h_lo = split(h.astype(F32) * gain)
        left = jnp.concatenate([low_hi, low_lo, e_hi, e_lo, h_hi, h_lo], axis=0)
        loads[2 * j].wait()
        k = jnp.dot(left, wk[part, :], preferred_element_type=F32)
        loads[2 * j + 1].wait()
        v = jnp.dot(left, wv[part, :], preferred_element_type=F32)
        acc_k[...] = k if j == 0 else acc_k[...] + k
        acc_v[...] = v if j == 0 else acc_v[...] + v
        raw = jnp.dot(spread[:, :192], h, preferred_element_type=F32)
        square = square + jnp.sum(raw * raw, axis=1, keepdims=True)

    def put(ref, full):
        hi, lo = split(full)
        ref[0] = hi
        ref[1] = lo

    def parts(acc):
        a = acc[0:64, :] + acc[64:128, :]
        b = acc[128:144, :] + acc[144:160, :]
        h = acc[160:352, :] + acc[352:544, :]
        h = jnp.concatenate([h, jnp.zeros((64, cols), F32)], axis=0)
        return a, b, lax.broadcasted_iota(jnp.int32, b.shape, 0), h

    kg = jnp.concatenate([kg_ref[...]] * heads, axis=1)
    pad = jnp.zeros((48, cols), F32)
    a, b, row, h = parts(acc_k)
    full = jnp.concatenate([a, jnp.where(row == 0, b, 0.0), pad], axis=0)
    put(akc, full)
    put(akg_ref, full * kg)
    put(akh_ref, h * kg)
    h_hi, h_lo = split(h)
    y = jnp.dot(spread, h_hi, preferred_element_type=F32) + jnp.dot(spread, h_lo, preferred_element_type=F32)
    s = lax.rsqrt(jnp.broadcast_to(square, (16, 128)) * (1.0 / width) + EPSILON)
    wide = jnp.where(lane == 70, s, 0.0)
    for head in range(heads):
        part = y[:, head * 128:(head + 1) * 128]
        mean = jnp.mean(part * part, axis=1, keepdims=True)
        wide = jnp.where(lane == 64 + head, s * lax.rsqrt(s * s * mean + EPSILON) * (LOG2E / math.sqrt(128.0)), wide)
    hi = wide.astype(BF).astype(F32)
    aux = jnp.where(lane == 80, level, hi + pltpu.roll(wide - hi, 8, 1))
    slots = jnp.concatenate([moved[0:8], aux[0:8]], axis=0)
    a, b, row, h = parts(acc_v)
    put(av_ref, jnp.concatenate([a, jnp.where(row < 2, b, 0.0), pad], axis=0))
    put(avh_ref, h)

    sigma = (STEPS - step) / STEPS
    bias = jnp.transpose(jnp.broadcast_to(bias_ref[...], (128, 128)))[:, 0:1]
    halo.wait_recv()
    lead = jnp.where(seq > 0, 1.0, 0.0)
    window = [jnp.where(lead > 0.5, early[0], jnp.zeros_like(early[0])),
              jnp.where(lead > 0.5, early[1], jnp.zeros_like(early[1])), feats_ref[0], feats_ref[1]]
    pixel = lax.broadcasted_iota(jnp.int32, (pixels, 256), 0)
    col = lax.broadcasted_iota(jnp.int32, (pixels, 256), 1)
    lines = [jnp.zeros((lw_ref.shape[0], 256), F32) for _ in range(4)]
    for t in range(frames):
        total = jnp.zeros((channels, pixels), F32)
        for tap in range(3):
            total = total + jnp.dot(cw_ref[tap], window[2 + t - tap], preferred_element_type=F32)
        total = total + bias
        hidden = (total * (1.0 / (1.0 + jnp.exp(-total)))).astype(BF)
        latent = jnp.dot(lw_ref[...], hidden, preferred_element_type=F32)
        noisy = ((1.0 - sigma) * latent + sigma * noise_ref[t].astype(F32)).astype(BF)
        for i in range(4):
            hit = (pixel % 4 == i) & (col == t * (pixels // 2) + grp * (pixels // 4) + pixel // 4)
            lines[i] = lines[i] + jnp.dot(noisy, jnp.where(hit, 1.0, 0.0).astype(BF), preferred_element_type=F32)
    mine[...] = jnp.concatenate(lines, axis=0).astype(BF)
    trade = send(3, mine, other, (1 - grp, seq))
    trade.start()
    piece_a.wait_recv()
    pass_a = send(4, far_ref.at[first_rows], far_ref.at[first_rows], (grp, sibling))
    pass_a.start()
    piece_b.wait_recv()
    pass_b = send(5, far_ref.at[second_rows], far_ref.at[second_rows], (grp, sibling))
    pass_b.start()
    trade.wait_recv()

    pt = mine[...].astype(F32) + other[...].astype(F32)
    row = lax.broadcasted_iota(jnp.int32, (64, 256), 0)
    tall = jnp.concatenate([pt, jnp.where(row == 0, 1.0, 0.0)], axis=0)
    px = jnp.transpose(tall)[:rows].astype(BF)
    p = px[:, :64]
    total = jnp.zeros((rows, 1), F32)
    total_row = jnp.zeros((8, rows), F32)
    ones = jnp.ones((8, chunk), BF)
    for j in range(width // chunk):
        part = slice(j * chunk, (j + 1) * chunk)
        x = jnp.dot(p, w_perm[:, part], preferred_element_type=F32) + wave[0:1, part]
        x_ref[:, part] = x
        x2 = x * x
        total = total + jnp.sum(x2, axis=1, keepdims=True)
        hi, lo = split(x2)
        total_row = total_row + lax.dot_general(ones, hi, NT, preferred_element_type=F32)
        total_row = total_row + lax.dot_general(ones, lo, NT, preferred_element_type=F32)
    s = lax.rsqrt(total * (1.0 / width) + EPSILON)
    s_row = lax.rsqrt(total_row * (1.0 / width) + EPSILON)
    y = jnp.dot(px, akc[0], preferred_element_type=F32) + jnp.dot(px, akc[1], preferred_element_type=F32)
    hi, lo = split(y * y)
    r8 = lax.broadcasted_iota(jnp.int32, (8, cols), 0)
    c8 = lax.broadcasted_iota(jnp.int32, (8, cols), 1)
    pick = jnp.where(c8 // 128 == r8, 1.0, 0.0).astype(BF)
    mean = (lax.dot_general(pick, hi, NT, preferred_element_type=F32)
            + lax.dot_general(pick, lo, NT, preferred_element_type=F32)) * (1.0 / 128)
    c = s_row * lax.rsqrt(s_row * s_row * mean + EPSILON) * (LOG2E / math.sqrt(128.0))
    r = lax.broadcasted_iota(jnp.int32, (8, rows), 0)
    both = jnp.where(r < heads, c, jnp.where(r == 6, s_row, 0.0))
    both = jnp.concatenate([both, jnp.zeros((8, 256 - rows), F32)], axis=1)
    hi8 = both.astype(BF).astype(F32)
    c16 = jnp.concatenate([hi8, both - hi8], axis=0)
    pay_ref[0:64, :] = pt[:, 0:128].astype(BF)
    lane32 = lax.broadcasted_iota(jnp.int32, (32, 128), 1)
    pay_ref[64:96, :] = jnp.where(lane32 < 64, pt[0:32, 128:256], pltpu.roll(pt[32:64, 128:256], 64, 1)).astype(BF)
    pay_ref[96:112, :] = c16[:, 0:128].astype(BF)
    pay_ref[112:128, :] = (c16[:, 128:256] + slots).astype(BF)
    for j in range(width // chunk):
        part = slice(j * chunk, (j + 1) * chunk)
        tok_ref[:, part] = (x_ref[:, part] * s * gain_ref[:, part]).astype(BF)

    pass_a.wait_recv()
    pass_b.wait_recv()
    for copy in (halo, piece_a, piece_b, trade, pass_a, pass_b):
        copy.wait_send()


def front(step_index, hist_level, feats, conv_weight, conv_bias, lat_weight, noise, hist, w_in, w_hist, gain, k_gain,
          w_key, w_value, w_out):
    rows = feats.shape[0] * feats.shape[2] // 2
    width, cols = w_key.shape
    vm = pl.BlockSpec(memory_space=pltpu.VMEM)
    sm = pl.BlockSpec(memory_space=pltpu.SMEM)
    hbm = pl.BlockSpec(memory_space=pl.ANY)
    dma = pltpu.SemaphoreType.DMA
    ops = jax.ShapeDtypeStruct((2, 128, cols), BF)
    big = jax.ShapeDtypeStruct((2, 256, cols), BF)
    return pl.pallas_call(
        front_kernel,
        out_shape=(jax.ShapeDtypeStruct((rows, width), BF), jax.ShapeDtypeStruct((128, 128), BF), ops, ops, big, big,
                   jax.ShapeDtypeStruct((w_out.shape[0], w_out.shape[1] // 2), BF)),
        in_specs=[sm, sm] + [vm] * 10 + [hbm] * 3,
        out_specs=(vm,) * 6 + (hbm,),
        scratch_shapes=[
            pltpu.VMEM(feats.shape, BF),
            pltpu.VMEM(w_key.shape, BF),
            pltpu.VMEM(w_value.shape, BF),
            pltpu.VMEM((544, cols), F32),
            pltpu.VMEM((544, cols), F32),
            pltpu.VMEM((rows, width), F32),
            pltpu.VMEM((2, 128, cols), BF),
            pltpu.VMEM((64, width), BF),
            pltpu.VMEM((8, width), F32),
            pltpu.VMEM((64, 256), BF),
            pltpu.VMEM((64, 256), BF),
            dma((6,)), dma((6,)), dma((6,)), dma((6,)),
        ],
        compiler_params=pltpu.CompilerParams(collective_id=1, has_side_effects=True, vmem_limit_bytes=60 << 20),
    )(step_index, hist_level, feats, conv_weight, conv_bias, lat_weight, noise, hist, w_in, w_hist, gain, k_gain,
      w_key, w_value, w_out)


def attend_kernel(chips, x_ref, tok_ref, wq_hbm, qg_ref, kg_ref, akg_ref, akh_ref, av_ref, avh_ref, live_ref, out_ref, theirs_ref,
                  g_ref, wq_ref, qop, qh, kt, vt, cs, acc, m_ref, hs, ax,
                  send_sem, recv_sem, fsend_sem, frecv_sem, osend_sem, orecv_sem, local_sem, wq_sem):
    grp = lax.axis_index("grp")
    seq = lax.axis_index("seq")
    core = seq % 2
    chip = seq // 2
    sibling = chip * 2 + 1 - core
    rows = tok_ref.shape[0]
    heads = wq_ref.shape[1] // 128
    group = kt.shape[1] // 384
    steps = chips // group

    def shift(k):
        z = (chip // 8 + k // 8) % 4
        x = (chip // 4 + k // 4) % 2
        y = (chip + k) % 4
        return (z * 2 + x) * 4 + y

    def back(k):
        z = (chip // 8 + 4 - k // 8) % 4
        x = (chip // 4 + k // 4) % 2
        y = (chip + 4 - k % 4) % 4
        return (z * 2 + x) * 4 + y

    load = pltpu.make_async_copy(wq_hbm, wq_ref, wq_sem)
    load.start()
    barrier = pltpu.get_barrier_semaphore()
    pl.semaphore_signal(barrier, inc=1, device_id=(grp, sibling), device_id_type=MESH)
    pl.semaphore_signal(barrier, inc=1, device_id=(1 - grp, seq), device_id_type=MESH)

    @pl.loop(1, chips)
    def _(k):
        pl.semaphore_signal(barrier, inc=1, device_id=(grp, shift(k) * 2 + core), device_id_type=MESH)

    pl.semaphore_wait(barrier, chips + 1)

    def direct(k):
        return pltpu.make_async_remote_copy(
            src_ref=x_ref, dst_ref=g_ref.at[seq], send_sem=send_sem.at[k], recv_sem=recv_sem.at[k],
            device_id=(grp, shift(k) * 2 + core), device_id_type=MESH)

    def forward(k):
        source = back(k) * 2 + core
        return pltpu.make_async_remote_copy(
            src_ref=g_ref.at[source], dst_ref=g_ref.at[source], send_sem=fsend_sem.at[k], recv_sem=frecv_sem.at[k],
            device_id=(grp, sibling), device_id_type=MESH)

    @pl.loop(1, chips)
    def _(k):
        direct(k).start()

    own = pltpu.make_async_copy(x_ref, g_ref.at[seq], local_sem)
    own.start()
    own.wait()
    forward(0).start()

    one_row = lax.broadcasted_iota(jnp.int32, (64, kt.shape[1]), 0)
    ones = jnp.where(one_row == 0, 1.0, 0.0).astype(BF)
    kt[64:128, :] = ones
    kt[192:256, :] = ones
    vt[80:128, :] = jnp.zeros((48, vt.shape[1]), BF)
    acc[...] = jnp.zeros_like(acc)
    m_ref[...] = jnp.full(m_ref.shape, LOW, F32)
    load.wait()
    for h in range(heads):
        sl = slice(h * rows, (h + 1) * rows)
        cols = slice(h * 128, (h + 1) * 128)
        q = jnp.dot(tok_ref[...], wq_ref[:, cols], preferred_element_type=F32)
        q = (q * lax.rsqrt(jnp.mean(q * q, axis=1, keepdims=True) + EPSILON) * qg_ref[...]).astype(BF)
        for ref, a_ref, n in ((qop, akg_ref, 128), (qh, akh_ref, 256)):
            qp = (lax.dot_general(q, a_ref[0, :, cols], NT, preferred_element_type=F32)
                  + lax.dot_general(q, a_ref[1, :, cols], NT, preferred_element_type=F32))
            hi, lo = split(qp)
            ref[sl, 0:n] = hi
            ref[sl, n:2 * n] = lo

    @pl.loop(1, group)
    def _(k):
        direct(k).wait_recv()
        forward(k).start()

    def absorb(h, s):
        sl = slice(h * rows, (h + 1) * rows)
        old = m_ref[sl, :]
        tiles = [s[:, j * 128:(j + 1) * 128] for j in range(s.shape[1] // 128)]
        top = functools.reduce(jnp.maximum, tiles)
        new = jnp.maximum(old, jnp.broadcast_to(jnp.max(top, axis=1, keepdims=True), old.shape))
        w = jnp.concatenate([jnp.exp2(t - new).astype(BF) for t in tiles], axis=1)
        m_ref[sl, :] = new
        return w, jnp.exp2(old - new)

    @pl.loop(0, steps)
    def _(i):
        for b in range(0, group, 2):
            places = []
            for k in (group * i + b, group * i + b + 1):
                forward(k).wait_recv()
                source = back(k) * 2
                places += [source, source + 1]
            cols = slice(b * 384, b * 384 + 768)
            unpack([g_ref[place] for place in places], kt.at[:, cols], vt.at[:, cols], cs.at[:, cols])

        def scores(h):
            return jnp.dot(qop[h * rows:(h + 1) * rows, :], kt[...], preferred_element_type=F32)

        def some(first, last):
            ahead = scores(first)
            for h in range(first, last):
                s = ahead
                if h + 1 < last:
                    ahead = scores(h + 1)
                sl = slice(h * rows, (h + 1) * rows)
                w, keep = absorb(h, s * cs[h:h + 1, :])
                acc[sl, :] = acc[sl, :] * keep + lax.dot_general(w, vt[...], NT, preferred_element_type=F32)

        some(0, heads // 2)

        @pl.when(i + 1 < steps)
        def _():
            for b in range(group):
                k = group * (i + 1) + b
                direct(k).wait_recv()
                forward(k).start()

        some(heads // 2, heads)

    @pl.loop(0, 2 * chips)
    def _(d):
        piece = pltpu.roll(g_ref[d, 112:128, :].astype(F32), 64, 1)
        spot = pl.ds(pl.multiple_of(d * 8, 8), 8)
        hs[spot, :] = piece[0:8]
        ax[spot, :] = piece[8:16]

    lane = lax.broadcasted_iota(jnp.int32, hs.shape, 1)
    level = ax[:, 16:17]
    size = ax[:, 6:7] + ax[:, 14:15]
    base = jnp.where(lane < 64, hs[...], 0.0)
    twice = base + pltpu.roll(base, 64, 1)
    first = jnp.where(level == jnp.where(lane < 64, 0.0, 1.0), twice, 0.0)
    second = jnp.where(level == 2.0, base, 0.0)
    kh = jnp.concatenate([first, second], axis=1).astype(BF)
    vh = jnp.concatenate([first * size, jnp.where(lane == 64, 1.0, second * size)], axis=1).astype(BF)
    across = jnp.transpose(ax[...])
    ch = across[0:8] + across[8:16]
    keys = kh.shape[0]
    owner = lax.broadcasted_iota(jnp.int32, (keys // 8, keys), 0)
    slot = lax.broadcasted_iota(jnp.int32, (keys // 8, keys), 1)
    counts = jnp.dot(jnp.broadcast_to(live_ref[...], (8, keys // 8)).astype(F32).astype(BF),
                     jnp.where(slot // 8 == owner, 1.0, 0.0).astype(BF), preferred_element_type=F32)
    hbias = jnp.where((slot[0:1] % 8).astype(F32) < counts[0:1], 0.0, LOW)

    def share(h):
        cols = slice(h * 128, (h + 1) * 128)
        return pltpu.make_async_remote_copy(
            src_ref=out_ref.at[:, cols], dst_ref=theirs_ref.at[:, cols], send_sem=osend_sem.at[h],
            recv_sem=orecv_sem.at[h], device_id=(1 - grp, seq), device_id_type=MESH)

    for h in range(heads):
        sl = slice(h * rows, (h + 1) * rows)
        cols = slice(h * 128, (h + 1) * 128)
        s = (lax.dot_general(qh[sl, 0:256], kh, NT, preferred_element_type=F32)
             + lax.dot_general(qh[sl, 256:512], kh, NT, preferred_element_type=F32))
        w, keep = absorb(h, s * ch[h:h + 1, :] + hbias)
        a = acc[sl, :] * keep
        b = jnp.dot(w, vh, preferred_element_type=F32)
        o = jnp.zeros((rows, 128), F32)
        for part, ref in ((a, av_ref), (b, avh_ref)):
            hi, lo = split(part)
            o = o + jnp.dot(hi, ref[0, :, cols], preferred_element_type=F32)
            o = o + jnp.dot(lo, ref[0, :, cols], preferred_element_type=F32)
            o = o + jnp.dot(hi, ref[1, :, cols], preferred_element_type=F32)
        out_ref[:, cols] = (o / (a[:, 66:67] + b[:, 192:193])).astype(BF)
        share(h).start()

    @pl.loop(0, chips)
    def _(k):
        forward(k).wait_send()

    @pl.loop(1, chips)
    def _(k):
        direct(k).wait_send()

    for h in range(heads):
        share(h).wait()


def attend(payload, tokens, w_query, q_gain, k_gain, akg, akh, av, avh, live, count):
    chips = count // 2
    rows = tokens.shape[0]
    cols = w_query.shape[1]
    tall = rows * cols // 128
    vm = pl.BlockSpec(memory_space=pltpu.VMEM)
    dma = pltpu.SemaphoreType.DMA
    return pl.pallas_call(
        functools.partial(attend_kernel, chips),
        out_shape=(jax.ShapeDtypeStruct((rows, cols), BF),) * 2,
        in_specs=[vm, vm, pl.BlockSpec(memory_space=pl.ANY)] + [vm] * 7,
        out_specs=(vm, vm),
        scratch_shapes=[
            pltpu.VMEM((count,) + payload.shape, BF),
            pltpu.VMEM(w_query.shape, BF),
            pltpu.VMEM((tall, 256), BF),
            pltpu.VMEM((tall, 512), BF),
            pltpu.VMEM((256, 1536), BF),
            pltpu.VMEM((128, 1536), BF),
            pltpu.VMEM((8, 1536), F32),
            pltpu.VMEM((tall, 128), F32),
            pltpu.VMEM((tall, 128), F32),
            pltpu.VMEM((count * 8, 128), F32),
            pltpu.VMEM((count * 8, 128), F32),
            dma((chips,)), dma((chips,)), dma((chips,)), dma((chips,)), dma((cols // 128,)), dma((cols // 128,)), dma, dma,
        ],
        compiler_params=pltpu.CompilerParams(collective_id=0, has_side_effects=True, vmem_limit_bytes=60 << 20),
    )(payload, tokens, w_query, q_gain, k_gain, akg, akh, av, avh, live)


def out_kernel(grp_ref, near_ref, theirs_ref, w_ref, far_ref, out_ref):
    out = jnp.dot(near_ref[...], w_ref[...], preferred_element_type=F32)
    out = out + jnp.dot(theirs_ref[...], far_ref[...], preferred_element_type=F32)
    out_ref[...] = out.astype(BF)


def project(near, theirs, w_out, far):
    rows, deep = near.shape
    half = far.shape[1]
    block = 256
    whole = pl.BlockSpec((rows, deep), lambda j, g: (0, 0))
    return pl.pallas_call(
        out_kernel,
        out_shape=jax.ShapeDtypeStruct((rows, half), BF),
        grid_spec=pltpu.PrefetchScalarGridSpec(
            num_scalar_prefetch=1,
            grid=(half // block,),
            in_specs=[
                whole, whole,
                pl.BlockSpec((deep, block), lambda j, g: (0, g[0] * (half // block) + j)),
                pl.BlockSpec((deep, block), lambda j, g: (0, j)),
            ],
            out_specs=pl.BlockSpec((rows, block), lambda j, g: (0, j)),
        ),
        compiler_params=pltpu.CompilerParams(vmem_limit_bytes=60 << 20),
    )(lax.axis_index("grp").astype(jnp.int32)[None], near, theirs, w_out, far)


def local(
    feats, conv_weight, conv_bias, latent_projection_weight, noise, step_index, hist, hist_level, hist_count,
    w_in, w_hist, norm_gain, w_query, w_key, w_value, q_gain, k_gain, w_out,
):
    width = w_in.shape[1]
    tokens, payload, akg, av, akh, avh, far = front(
        step_index, hist_level, feats, conv_weight, conv_bias[None], latent_projection_weight, noise, hist, w_in,
        w_hist.reshape(-1, width), norm_gain[None], k_gain[None], w_key, w_value, w_out)
    near, theirs = attend(
        payload, tokens, w_query, q_gain[None], k_gain[None], akg, akh, av, avh, hist_count[None], lax.axis_size("seq"))
    return project(near, theirs, w_out, far)


def solution(mesh):
    placed = (
        P("seq", None, "grp"), P(), P(), P(), P("seq", None, "grp"), P(), P("seq", None), P("seq"), P(), P(), P(), P(),
        P(None, "grp"), P(None, "grp"), P(None, "grp"), P(), P(), P("grp", None),
    )
    return jax.shard_map(local, mesh=mesh, in_specs=placed, out_specs=P("seq", "grp"), check_vma=False)
```

time: 370 us -> 91.4 us (0.25)
  waiting for transfers between devices: 191 us -> 0 us
  Pallas kernels: 0 us -> 88 us
  matrix products: 78.9 us -> 0 us
  local copies, waits for them, and re-layouts: 55.3 us -> 1.65 us
  other arithmetic: 25 us -> 0 us
  between operations: 14 us -> 0.67 us
    all_gather x3 -> x0, waiting for transfers between devices: 164 us -> none  [the longest x1 96.6 us: local(): key_piece = lax.all_gather(flattened_keys, 'seq', axis=0, tiled=True)]
    pallas_call x0 -> x3, Pallas kernels: none -> 88 us  [the longest x1 58.4 us: attend(): pl.pallas_call(functools.partial(attend_kernel, chips), out_shape=(jax.Sh...]
    dot_general x13 -> x0, matrix products: 78.9 us -> none  [the longest x1 27.5 us: local(): jnp.einsum('qhd,khd->hqk', query, key_heads, preferred_element_type=jnp.f...]
    all_gather x2 -> x0, local copies, waits for them, and re-layouts: 47.6 us -> none  [the longest x1 23.8 us: local(): key_piece = lax.all_gather(flattened_keys, 'seq', axis=0, tiled=True)]
    reduce_scatter x1 -> x0, waiting for transfers between devices: 24.3 us -> none  [local(): lax.psum_scatter(partial_out.astype(jnp.bfloat16), 'grp', scatter_dimensi...]
    reduce_sum x3 -> x0, other arithmetic: 22.3 us -> none  [the longest x1 21.4 us: local(): new_sum = jnp.sum(soft, axis=-1)]
    unnamed x17 -> x1, local copies, waits for them, and re-layouts: 6.78 us -> 1.65 us
  transfers between devices with their start and end apart: 5 -> 0, of which waited for: 5 -> 0; matrix products, arithmetic and copies ran while one was open for 26% -> 0% of each run, Pallas kernels for 0% -> 0%
where the time goes in v2:
time: 91.4 us; the launch traced here: 90.3 us
  Pallas kernels  88 us (96%)
  local copies, waits for them, and re-layouts  1.65 us (2%)
    pallas_call x1, Pallas kernels, attend(): pl.pallas_call(functools.partial(attend_kernel, chips), out_shape=(jax.Sh...  58.4 us
    pallas_call x1, Pallas kernels, front(): pl.pallas_call(front_kernel, out_shape=(jax.ShapeDtypeStruct((rows, width...  23.6 us
    pallas_call x1, Pallas kernels, project(): pl.pallas_call(out_kernel, out_shape=jax.ShapeDtypeStruct((rows, half), B...  6.01 us

profile of v2, /device:TPU:4, one launch (start us, length us, event | category | flops | bytes accessed | tf_op | source)
XLA Modules:
  0.0 90.3 jit_solution(17058668784678184292)
XLA Ops:
  0.0 1.7 %copy.19.feats_ref = bf16[2,128,192]{2,1,0:T(8,128)(2,1)} copy(bf16[2,128,192]{1,2,0:T(8,128)(2,1)} %param.18) | data formatting | bytes 196608 | tf_op args[0]
  2.3 23.6 %shard_map.172 = (bf16[192,3072]{1,0:T(8,128)(2,1)}, bf16[128,128]{1,0:T(8,128)(2,1)}, bf16[2,128,768]{2,1,0:T(8,128)(2,1)}, bf16[2,128,768]{2,1,0:T(8,128)(2,1)...) custom-call(s32[1]{0:T(128)S(6)} %copy.20.step_ref, s32[8]{0:T(128)} %level_ref.1, ...), custom_call_target="tpu_custom_call" | custom-call | tf_op jit(solution)/shard_map/pallas_call | solution.py:271
  25.9 58.4 %shard_map.173 = (bf16[192,768]{1,0:T(8,128)(2,1)}, bf16[192,768]{1,0:T(8,128)(2,1)}) custom-call(bf16[128,128]{1,0:T(8,128)(2,1)} %get-tuple-element.14.x_ref, bf16[192,3072]{1,0:T(8,128)(2,1)} %get-tuple-element.15.tok_ref, bf16[3072,768]{1,0:T(8,128)(2,1)} %wq_hbm.1, f32[1,128]{1,0:T(1,128)} %bitcast.12, f32[1,128]{1,0:T(1,128)} %bitcast.10, ...), custom_call_target="tpu_custom_call" | custom-call | tf_op jit(solution)/shard_map/pallas_call | solution.py:490
  84.3 6.0 %shard_map.174 = bf16[192,1536]{1,0:T(8,128)(2,1)} custom-call(s32[1]{0:T(128)} %bitcast.grp_ref, bf16[192,768]{1,0:T(8,128)(2,1)} %get-tuple-element.20.near_ref, bf16[192,768]{1,0:T(8,128)(2,1)} %get-tuple-element.21.theirs_ref, bf16[768,3072]{1,0:T(8,128)(2,1)} %w_ref.1, bf16[768,1536]{1,0:T(8,128)(2,1)} %get-tuple-element.22.far_ref), custom_call_target="tpu_custom_call" | custom-call | tf_op jit(solution)/shard_map/pallas_call | solution.py:524

commit v3 on v2

v3 whole, which is shorter than its diff:
```python
import functools
import math

import jax
import jax.numpy as jnp
from jax import lax
from jax.experimental import pallas as pl
from jax.experimental.pallas import tpu as pltpu
from jax.sharding import PartitionSpec as P

STEPS = 50
EPSILON = 1e-06
LOG2E = math.log2(math.e)
MESH = pl.DeviceIdType.MESH
BF = jnp.bfloat16
F32 = jnp.float32
LOW = -1e30


def split(x):
    hi = x.astype(BF)
    return hi, (x - hi.astype(F32)).astype(BF)


def unpack(block, kt_ref, vt_ref, c_ref):
    lane = lax.broadcasted_iota(jnp.int32, (64, 128), 1)
    lane16 = lax.broadcasted_iota(jnp.int32, (16, 128), 1)
    for pair in range(2):
        first, second = block[2 * pair].astype(F32), block[2 * pair + 1].astype(F32)

        def rest(x):
            low = x[64:96]
            return jnp.concatenate([low, pltpu.roll(low, 64, 1)], axis=0)

        tails = jnp.where(lane < 64, rest(first), pltpu.roll(rest(second), 64, 1))
        tail16 = jnp.where(lane16 < 64, first[112:128], pltpu.roll(second[112:128], 64, 1))
        parts = [
            (first[0:64], first[96:112]),
            (tails, tail16),
            (second[0:64], second[96:112]),
        ]
        for tile, (p, c16) in enumerate(parts):
            cols = slice((3 * pair + tile) * 128, (3 * pair + tile + 1) * 128)
            scales = c16[0:8] + c16[8:16]
            c_ref[:, cols] = scales
            pb = p.astype(BF)
            kt_ref[0:64, cols] = pb
            kt_ref[128:192, cols] = pb
            s_row = scales[6:7]
            vt_ref[0:64, cols] = (p * s_row).astype(BF)
            s_hi = c16[6:7]
            s_lo = c16[14:15]
            row = lax.broadcasted_iota(jnp.int32, (16, 128), 0)
            extra = jnp.where(row == 0, s_hi, jnp.where(row == 1, s_lo, jnp.where(row == 2, 1.0, 0.0)))
            vt_ref[64:80, cols] = extra.astype(BF)


NT = (((1,), (1,)), ((), ()))


def section_kernel(step_ref, level_ref, feats_ref, cw_ref, bias_ref, lw_ref, noise_ref, hist_ref, w_in_ref, wh_ref,
                   gain_ref, kg_ref, qg_ref, live_ref, wq_hbm, wk_hbm, wv_hbm, wout_hbm, out_ref,
                   early, wk, wv, acc_k, acc_v, x_ref, akc, w_perm, wave, mine, other, far_ref, near_ref,
                   tok_ref, pay_ref, lefts, akg_ref, av_ref, akh_ref, avh_ref,
                   g_ref, wq_ref, qop, qh, kt, vt, cs, acc, m_ref, hs, ax, own, theirs,
                   wk_sem, wv_sem, tsend_sem, trecv_sem, load_sem,
                   send_sem, recv_sem, fsend_sem, frecv_sem, osend_sem, orecv_sem):
    grp = lax.axis_index("grp")
    seq = lax.axis_index("seq")
    count = lax.axis_size("seq")
    core = seq % 2
    sibling = seq + 1 - 2 * core
    across = seq + 8 - 16 * ((seq // 8) % 2)
    after, before = (seq + 1) % count, (seq + count - 1) % count
    chip = seq // 2
    chips = count // 2
    frames, pixels, channels = feats_ref.shape
    rows, width = tok_ref.shape
    group = kt.shape[1] // 384
    steps = chips // group

    def shift(k):
        z = (chip // 8 + (k // 4) % 4) % 4
        x = (chip // 4 + k // 16) % 2
        y = (chip + k) % 4
        return (z * 2 + x) * 4 + y

    def back(k):
        z = (chip // 8 + 4 - (k // 4) % 4) % 4
        x = (chip // 4 + k // 16) % 2
        y = (chip + 4 - k % 4) % 4
        return (z * 2 + x) * 4 + y

    cols = kg_ref.shape[1] * 6
    heads = cols // 128
    chunk = 512
    quarter = far_ref.shape[0] // 4
    half = far_ref.shape[1]

    def chunk_load(source, into, sem, j):
        part = pl.ds(j * chunk, chunk)
        return pltpu.make_async_copy(source.at[part], into.at[part], sem.at[j])

    key_loads = [chunk_load(wk_hbm, wk, wk_sem, j) for j in range(width // chunk)]
    value_loads = [chunk_load(wv_hbm, wv, wv_sem, j) for j in range(width // chunk)]
    for load in key_loads + value_loads:
        load.start()

    barrier = pltpu.get_barrier_semaphore()
    for there in ((1 - grp, seq), (1 - grp, across), (grp, sibling), (grp, after), (grp, before)):
        pl.semaphore_signal(barrier, inc=1, device_id=there, device_id_type=MESH)

    plane = chips // 2

    @pl.loop(1, plane + 1)
    def _(k):
        pl.semaphore_signal(barrier, inc=1, device_id=(grp, shift(k) * 2 + core), device_id_type=MESH)

    pl.semaphore_wait(barrier, plane + 5)

    def send(n, source, into, there):
        return pltpu.make_async_remote_copy(
            src_ref=source, dst_ref=into, send_sem=tsend_sem.at[n], recv_sem=trecv_sem.at[n],
            device_id=there, device_id_type=MESH)

    halo = send(0, feats_ref, early, (grp, after))
    halo.start()
    first_rows = pl.ds(pl.multiple_of(2 * core * quarter, quarter), quarter)
    second_rows = pl.ds(pl.multiple_of((2 * core + 1) * quarter, quarter), quarter)
    far_cols = pl.ds(pl.multiple_of((1 - grp) * half, half), half)
    piece_a = send(1, wout_hbm.at[first_rows, far_cols], far_ref.at[first_rows], (1 - grp, seq))
    piece_b = send(2, wout_hbm.at[second_rows, far_cols], far_ref.at[second_rows], (1 - grp, across))

    step = step_ref[0].astype(F32)
    place = lax.broadcasted_iota(jnp.int32, (8, width), 1)
    turn = jnp.where(place < width // 2, place, place - width // 2).astype(F32)
    angle = step * jnp.exp(turn * (-math.log(10000.0) / (width // 2)))
    wave[...] = jnp.where(place < width // 2, jnp.cos(angle), jnp.sin(angle))
    lane = lax.broadcasted_iota(jnp.int32, (16, 128), 1)
    line = lax.broadcasted_iota(jnp.int32, (16, 128), 0)
    level = jnp.zeros((16, 128), F32)
    for r in range(8):
        level = jnp.where(line == r, level_ref[r].astype(F32), level)
    base = jnp.concatenate([hist_ref[...].astype(F32), jnp.zeros((8, 64), F32)], axis=1)
    base = jnp.concatenate([base, jnp.zeros((8, 128), F32)], axis=0)
    moved = pltpu.roll(base, 64, 1)
    spread = jnp.concatenate([
        jnp.where(level == jnp.where(lane < 64, 0.0, 1.0), base + moved, 0.0),
        jnp.where(level == 2.0, base, 0.0)], axis=1).astype(BF)
    r64 = lax.broadcasted_iota(jnp.int32, (64, 64), 0)
    c64 = lax.broadcasted_iota(jnp.int32, (64, 64), 1)
    order = jnp.where(c64 == (r64 % 16) * 4 + r64 // 16, 1.0, 0.0).astype(BF)

    square = jnp.zeros((16, 1), F32)
    for j in range(width // chunk):
        part = slice(j * chunk, (j + 1) * chunk)
        gain = gain_ref[:, part]
        low = jnp.dot(order, w_in_ref[:, part], preferred_element_type=F32)
        w_perm[:, part] = low.astype(BF)
        low_hi, low_lo = split(low * gain)
        e_hi, e_lo = split(jnp.concatenate([wave[:, part]] * 2, axis=0) * gain)
        raw = jnp.dot(spread[:, :192], wh_ref[:, part], preferred_element_type=F32)
        square = square + jnp.sum(raw * raw, axis=1, keepdims=True)
        r_hi, r_lo = split(raw * gain)
        base_rows = jnp.concatenate([low_hi, low_lo, e_hi, e_lo], axis=0)
        lefts[:, part] = base_rows
        key_loads[j].wait()
        k = jnp.dot(jnp.concatenate([base_rows, r_hi, r_lo], axis=0), wk[part, :], preferred_element_type=F32)
        acc_k[0:192, :] = k if j == 0 else acc_k[0:192, :] + k

    def put(ref, full):
        hi, lo = split(full)
        ref[0] = hi
        ref[1] = lo

    def low_parts(acc):
        a = acc[0:64, :] + acc[64:128, :]
        b = acc[128:144, :] + acc[144:160, :]
        return a, b, lax.broadcasted_iota(jnp.int32, b.shape, 0)

    kg = jnp.concatenate([kg_ref[...]] * heads, axis=1)
    pad = jnp.zeros((48, cols), F32)
    a, b, row = low_parts(acc_k)
    full = jnp.concatenate([a, jnp.where(row == 0, b, 0.0), pad], axis=0)
    put(akc, full)
    put(akg_ref, full * kg)
    y = acc_k[160:176, :] + acc_k[176:192, :]
    s = lax.rsqrt(jnp.broadcast_to(square, (16, 128)) * (1.0 / width) + EPSILON)
    wide = jnp.where(lane == 70, s, 0.0)
    for head in range(heads):
        part = y[:, head * 128:(head + 1) * 128]
        mean = jnp.mean(part * part, axis=1, keepdims=True)
        wide = jnp.where(lane == 64 + head, s * lax.rsqrt(s * s * mean + EPSILON) * (LOG2E / math.sqrt(128.0)), wide)
    hi = wide.astype(BF).astype(F32)
    aux = jnp.where(lane == 80, level, hi + pltpu.roll(wide - hi, 8, 1))
    slots = jnp.concatenate([moved[0:8], aux[0:8]], axis=0)

    load_query = pltpu.make_async_copy(wq_hbm, wq_ref, load_sem.at[0])
    load_query.start()
    near_cols = pl.ds(pl.multiple_of(grp * half, half), half)
    load_near = pltpu.make_async_copy(wout_hbm.at[:, near_cols], near_ref, load_sem.at[1])
    load_near.start()
    sigma = (STEPS - step) / STEPS
    bias = jnp.transpose(jnp.broadcast_to(bias_ref[...], (128, 128)))[:, 0:1]
    halo.wait_recv()
    lead = jnp.where(seq > 0, 1.0, 0.0)
    window = [jnp.where(lead > 0.5, early[0], jnp.zeros_like(early[0])),
              jnp.where(lead > 0.5, early[1], jnp.zeros_like(early[1])), feats_ref[0], feats_ref[1]]
    pixel = lax.broadcasted_iota(jnp.int32, (pixels, 256), 0)
    col = lax.broadcasted_iota(jnp.int32, (pixels, 256), 1)
    lines = [jnp.zeros((lw_ref.shape[0], 256), F32) for _ in range(4)]
    for t in range(frames):
        total = jnp.zeros((channels, pixels), F32)
        for tap in range(3):
            total = total + lax.dot_general(cw_ref[tap], window[2 + t - tap], NT, preferred_element_type=F32)
        total = total + bias
        hidden = (total * (1.0 / (1.0 + jnp.exp(-total)))).astype(BF)
        latent = jnp.dot(lw_ref[...], hidden, preferred_element_type=F32)
        noisy = ((1.0 - sigma) * latent + sigma * noise_ref[t].astype(F32)).astype(BF)
        for i in range(4):
            hit = (pixel % 4 == i) & (col == t * (pixels // 2) + grp * (pixels // 4) + pixel // 4)
            lines[i] = lines[i] + jnp.dot(noisy, jnp.where(hit, 1.0, 0.0).astype(BF), preferred_element_type=F32)
    mine[...] = jnp.concatenate(lines, axis=0).astype(BF)
    trade = send(3, mine, other, (1 - grp, seq))
    trade.start()
    pass_a = send(4, far_ref.at[first_rows], far_ref.at[first_rows], (grp, sibling))
    pass_b = send(5, far_ref.at[second_rows], far_ref.at[second_rows], (grp, sibling))
    trade.wait_recv()

    pt = mine[...].astype(F32) + other[...].astype(F32)
    row = lax.broadcasted_iota(jnp.int32, (64, 256), 0)
    tall = jnp.concatenate([pt, jnp.where(row == 0, 1.0, 0.0)], axis=0)
    px = jnp.transpose(tall)[:rows].astype(BF)
    p = px[:, :64]
    total = jnp.zeros((rows, 1), F32)
    total_row = jnp.zeros((8, rows), F32)
    ones = jnp.ones((8, chunk), BF)
    for j in range(width // chunk):
        part = slice(j * chunk, (j + 1) * chunk)
        x = jnp.dot(p, w_perm[:, part], preferred_element_type=F32) + wave[0:1, part]
        x_ref[:, part] = x
        x2 = x * x
        total = total + jnp.sum(x2, axis=1, keepdims=True)
        hi, lo = split(x2)
        total_row = total_row + lax.dot_general(ones, hi, NT, preferred_element_type=F32)
        total_row = total_row + lax.dot_general(ones, lo, NT, preferred_element_type=F32)
    s = lax.rsqrt(total * (1.0 / width) + EPSILON)
    s_row = lax.rsqrt(total_row * (1.0 / width) + EPSILON)
    y = jnp.dot(px, akc[0], preferred_element_type=F32) + jnp.dot(px, akc[1], preferred_element_type=F32)
    hi, lo = split(y * y)
    r8 = lax.broadcasted_iota(jnp.int32, (8, cols), 0)
    c8 = lax.broadcasted_iota(jnp.int32, (8, cols), 1)
    pick = jnp.where(c8 // 128 == r8, 1.0, 0.0).astype(BF)
    mean = (lax.dot_general(pick, hi, NT, preferred_element_type=F32)
            + lax.dot_general(pick, lo, NT, preferred_element_type=F32)) * (1.0 / 128)
    c = s_row * lax.rsqrt(s_row * s_row * mean + EPSILON) * (LOG2E / math.sqrt(128.0))
    r = lax.broadcasted_iota(jnp.int32, (8, rows), 0)
    both = jnp.where(r < heads, c, jnp.where(r == 6, s_row, 0.0))
    both = jnp.concatenate([both, jnp.zeros((8, 256 - rows), F32)], axis=1)
    hi8 = both.astype(BF).astype(F32)
    c16 = jnp.concatenate([hi8, both - hi8], axis=0)
    pay_ref[0:64, :] = pt[:, 0:128].astype(BF)
    lane32 = lax.broadcasted_iota(jnp.int32, (32, 128), 1)
    pay_ref[64:96, :] = jnp.where(lane32 < 64, pt[0:32, 128:256], pltpu.roll(pt[32:64, 128:256], 64, 1)).astype(BF)
    pay_ref[96:112, :] = c16[:, 0:128].astype(BF)
    pay_ref[112:128, :] = (c16[:, 128:256] + slots).astype(BF)
    def direct(k):
        return pltpu.make_async_remote_copy(
            src_ref=pay_ref, dst_ref=g_ref.at[seq], send_sem=send_sem.at[k], recv_sem=recv_sem.at[k],
            device_id=(grp, shift(k) * 2 + core), device_id_type=MESH)

    def forward(k):
        source = back(k) * 2 + core
        return pltpu.make_async_remote_copy(
            src_ref=g_ref.at[source], dst_ref=g_ref.at[source], send_sem=fsend_sem.at[k], recv_sem=frecv_sem.at[k],
            device_id=(grp, sibling), device_id_type=MESH)

    facing = back(plane) * 2 + core

    def relay(k):
        return pltpu.make_async_remote_copy(
            src_ref=g_ref.at[facing], dst_ref=g_ref.at[facing], send_sem=send_sem.at[k], recv_sem=recv_sem.at[k],
            device_id=(grp, shift(k - plane) * 2 + core), device_id_type=MESH)

    direct(plane).start()

    @pl.loop(1, plane)
    def _(k):
        direct(k).start()

    here = pltpu.make_async_copy(pay_ref, g_ref.at[seq], load_sem.at[2])
    here.start()
    here.wait()
    forward(0).start()

    for j in range(width // chunk):
        part = slice(j * chunk, (j + 1) * chunk)
        tok_ref[:, part] = (x_ref[:, part] * s * gain_ref[:, part]).astype(BF)

    one_row = lax.broadcasted_iota(jnp.int32, (64, kt.shape[1]), 0)
    ones = jnp.where(one_row == 0, 1.0, 0.0).astype(BF)
    kt[64:128, :] = ones
    kt[192:256, :] = ones
    vt[80:128, :] = jnp.zeros((48, vt.shape[1]), BF)
    acc[...] = jnp.zeros_like(acc)
    m_ref[...] = jnp.full(m_ref.shape, LOW, F32)
    direct(plane).wait_recv()
    forward(plane).start()

    @pl.loop(plane + 1, chips)
    def _(k):
        relay(k).start()

    for j in range(width // chunk):
        part = slice(j * chunk, (j + 1) * chunk)
        h_hi, h_lo = split(wh_ref[:, part].astype(F32) * gain_ref[:, part])
        both_h = jnp.concatenate([h_hi, h_lo], axis=0)
        k = jnp.dot(both_h, wk[part, :], preferred_element_type=F32)
        value_loads[j].wait()
        v = jnp.dot(jnp.concatenate([lefts[:, part], both_h], axis=0), wv[part, :], preferred_element_type=F32)
        acc_k[0:384, :] = k if j == 0 else acc_k[0:384, :] + k
        acc_v[...] = v if j == 0 else acc_v[...] + v
    pad_h = jnp.zeros((64, cols), F32)
    put(akh_ref, jnp.concatenate([acc_k[0:192, :] + acc_k[192:384, :], pad_h], axis=0) * kg)
    a, b, row = low_parts(acc_v)
    put(av_ref, jnp.concatenate([a, jnp.where(row < 2, b, 0.0), pad], axis=0))
    put(avh_ref, jnp.concatenate([acc_v[160:352, :] + acc_v[352:544, :], pad_h], axis=0))

    @pl.loop(1, group)
    def _(k):
        direct(k).wait_recv()
        forward(k).start()

    load_query.wait()
    for h in range(heads):
        sl = slice(h * rows, (h + 1) * rows)
        cols = slice(h * 128, (h + 1) * 128)
        q = jnp.dot(tok_ref[...], wq_ref[:, cols], preferred_element_type=F32)
        q = (q * lax.rsqrt(jnp.mean(q * q, axis=1, keepdims=True) + EPSILON) * qg_ref[...]).astype(BF)
        for ref, a_ref, n in ((qop, akg_ref, 128), (qh, akh_ref, 256)):
            qp = (lax.dot_general(q, a_ref[0, :, cols], NT, preferred_element_type=F32)
                  + lax.dot_general(q, a_ref[1, :, cols], NT, preferred_element_type=F32))
            hi, lo = split(qp)
            ref[sl, 0:n] = hi
            ref[sl, n:2 * n] = lo

    @pl.loop(group, 2 * group)
    def _(k):
        direct(k).wait_recv()
        forward(k).start()

    def absorb(h, s):
        sl = slice(h * rows, (h + 1) * rows)
        old = m_ref[sl, :]
        tiles = [s[:, j * 128:(j + 1) * 128] for j in range(s.shape[1] // 128)]
        top = functools.reduce(jnp.maximum, tiles)
        new = jnp.maximum(old, jnp.broadcast_to(jnp.max(top, axis=1, keepdims=True), old.shape))
        w = jnp.concatenate([jnp.exp2(t - new).astype(BF) for t in tiles], axis=1)
        m_ref[sl, :] = new
        return w, jnp.exp2(old - new)

    def take(i):
        for b in range(0, group, 2):
            places = []
            for k in (group * i + b, group * i + b + 1):
                forward(k).wait_recv()
                source = back(k) * 2
                places += [source, source + 1]
            lot = slice(b * 384, b * 384 + 768)
            unpack([g_ref[place] for place in places], kt.at[:, lot], vt.at[:, lot], cs.at[:, lot])

    def scores(h):
        return jnp.dot(qop[h * rows:(h + 1) * rows, :], kt[...], preferred_element_type=F32)

    @pl.loop(0, steps - 1)
    def _(i):
        take(i)

        def some(first, last):
            ahead = scores(first)
            for h in range(first, last):
                s = ahead
                if h + 1 < last:
                    ahead = scores(h + 1)
                sl = slice(h * rows, (h + 1) * rows)
                w, keep = absorb(h, s * cs[h:h + 1, :])
                acc[sl, :] = acc[sl, :] * keep + lax.dot_general(w, vt[...], NT, preferred_element_type=F32)

        some(0, heads // 2)

        @pl.when((i + 2 < steps) & (i + 2 != steps // 2))
        def _():
            for b in range(group):
                k = group * (i + 2) + b
                direct(k).wait_recv()
                forward(k).start()

        @pl.when(i + 2 == steps // 2)
        def _():
            for b in range(1, group):
                k = plane + b
                direct(k).wait_recv()
                forward(k).start()

        @pl.when(i == 0)
        def _():
            piece_a.start()
            piece_b.start()

        @pl.when(i == steps - 2)
        def _():
            piece_a.wait_recv()
            pass_a.start()
            piece_b.wait_recv()
            pass_b.start()

        some(heads // 2, heads)

    take(steps - 1)

    @pl.loop(0, chips // 4)
    def _(n):
        for b in range(8):
            piece = pltpu.roll(g_ref[n * 8 + b, 112:128, :].astype(F32), 64, 1)
            spot = pl.ds(pl.multiple_of(n * 64 + b * 8, 8), 8)
            hs[spot, :] = piece[0:8]
            ax[spot, :] = piece[8:16]

    lane = lax.broadcasted_iota(jnp.int32, hs.shape, 1)
    level = ax[:, 16:17]
    size = ax[:, 6:7] + ax[:, 14:15]
    base = jnp.where(lane < 64, hs[...], 0.0)
    twice = base + pltpu.roll(base, 64, 1)
    first = jnp.where(level == jnp.where(lane < 64, 0.0, 1.0), twice, 0.0)
    second = jnp.where(level == 2.0, base, 0.0)
    kh = jnp.concatenate([first, second], axis=1).astype(BF)
    vh = jnp.concatenate([first * size, jnp.where(lane == 64, 1.0, second * size)], axis=1).astype(BF)
    across = jnp.transpose(ax[...])
    ch = across[0:8] + across[8:16]
    keys = kh.shape[0]
    owner = lax.broadcasted_iota(jnp.int32, (keys // 8, keys), 0)
    slot = lax.broadcasted_iota(jnp.int32, (keys // 8, keys), 1)
    counts = jnp.dot(jnp.broadcast_to(live_ref[...], (8, keys // 8)).astype(F32).astype(BF),
                     jnp.where(slot // 8 == owner, 1.0, 0.0).astype(BF), preferred_element_type=F32)
    hbias = jnp.where((slot[0:1] % 8).astype(F32) < counts[0:1], 0.0, LOW)

    def hist_scores(h):
        sl = slice(h * rows, (h + 1) * rows)
        return (lax.dot_general(qh[sl, 0:256], kh, NT, preferred_element_type=F32)
                + lax.dot_general(qh[sl, 256:512], kh, NT, preferred_element_type=F32))

    def share(h):
        lot = slice(h * 128, (h + 1) * 128)
        return pltpu.make_async_remote_copy(
            src_ref=own.at[:, lot], dst_ref=theirs.at[:, lot], send_sem=osend_sem.at[h],
            recv_sem=orecv_sem.at[h], device_id=(1 - grp, seq), device_id_type=MESH)

    def both_scores(h):
        return scores(h), hist_scores(h)

    ahead = both_scores(0)
    for h in range(heads):
        s, t = ahead
        if h + 1 < heads:
            ahead = both_scores(h + 1)
        sl = slice(h * rows, (h + 1) * rows)
        lot = slice(h * 128, (h + 1) * 128)
        wide_s = jnp.concatenate([s * cs[h:h + 1, :], t * ch[h:h + 1, :] + hbias], axis=1)
        w, keep = absorb(h, wide_s)
        n = s.shape[1]
        a = acc[sl, :] * keep + lax.dot_general(w[:, :n], vt[...], NT, preferred_element_type=F32)
        b = jnp.dot(w[:, n:], vh, preferred_element_type=F32)
        if h > 0:
            share(h - 1).start()
        o = jnp.zeros((rows, 128), F32)
        for value, weight in ((a, av_ref), (b, avh_ref)):
            hi, lo = split(value)
            o = o + jnp.dot(hi, weight[0, :, lot], preferred_element_type=F32)
            o = o + jnp.dot(lo, weight[0, :, lot], preferred_element_type=F32)
            o = o + jnp.dot(hi, weight[1, :, lot], preferred_element_type=F32)
        own[:, lot] = (o / (a[:, 66:67] + b[:, 192:193])).astype(BF)
    share(heads - 1).start()

    load_near.wait()
    for j in range(half // chunk):
        part = slice(j * chunk, (j + 1) * chunk)
        x_ref[:, part] = jnp.dot(own[...], near_ref[:, part], preferred_element_type=F32)
    pass_a.wait_recv()
    pass_b.wait_recv()
    for h in range(heads):
        share(h).wait_recv()
    for j in range(half // chunk):
        part = slice(j * chunk, (j + 1) * chunk)
        out_ref[:, part] = (x_ref[:, part]
                            + jnp.dot(theirs[...], far_ref[:, part], preferred_element_type=F32)).astype(BF)

    @pl.loop(0, chips)
    def _(k):
        forward(k).wait_send()

    @pl.loop(1, plane + 1)
    def _(k):
        direct(k).wait_send()

    @pl.loop(plane + 1, chips)
    def _(k):
        relay(k).wait_send()

    for h in range(heads):
        share(h).wait_send()
    for copy in (halo, piece_a, piece_b, trade, pass_a, pass_b):
        copy.wait_send()


def section(step_index, hist_level, feats, conv_weight, conv_bias, lat_weight, noise, hist, w_in, w_hist, gain, k_gain,
            q_gain, live, w_query, w_key, w_value, w_out):
    rows = feats.shape[0] * feats.shape[1] // 2
    width, cols = w_key.shape
    heads = cols // 128
    tall = rows * heads
    count = live.shape[1]
    chips = count // 2
    half = w_out.shape[1] // 2
    vm = pl.BlockSpec(memory_space=pltpu.VMEM)
    sm = pl.BlockSpec(memory_space=pltpu.SMEM)
    hbm = pl.BlockSpec(memory_space=pl.ANY)
    dma = pltpu.SemaphoreType.DMA
    return pl.pallas_call(
        section_kernel,
        out_shape=jax.ShapeDtypeStruct((rows, half), BF),
        in_specs=[sm, sm] + [vm] * 12 + [hbm] * 4,
        out_specs=vm,
        scratch_shapes=[
            pltpu.VMEM(feats.shape, BF),
            pltpu.VMEM(w_key.shape, BF),
            pltpu.VMEM(w_value.shape, BF),
            pltpu.VMEM((544, cols), F32),
            pltpu.VMEM((544, cols), F32),
            pltpu.VMEM((rows, width), F32),
            pltpu.VMEM((2, 128, cols), BF),
            pltpu.VMEM((64, width), BF),
            pltpu.VMEM((8, width), F32),
            pltpu.VMEM((64, 256), BF),
            pltpu.VMEM((64, 256), BF),
            pltpu.VMEM((w_out.shape[0], half), BF),
            pltpu.VMEM((w_out.shape[0], half), BF),
            pltpu.VMEM((rows, width), BF),
            pltpu.VMEM((128, 128), BF),
            pltpu.VMEM((160, width), BF),
            pltpu.VMEM((2, 128, cols), BF),
            pltpu.VMEM((2, 128, cols), BF),
            pltpu.VMEM((2, 256, cols), BF),
            pltpu.VMEM((2, 256, cols), BF),
            pltpu.VMEM((count, 128, 128), BF),
            pltpu.VMEM(w_query.shape, BF),
            pltpu.VMEM((tall, 256), BF),
            pltpu.VMEM((tall, 512), BF),
            pltpu.VMEM((256, 1536), BF),
            pltpu.VMEM((128, 1536), BF),
            pltpu.VMEM((8, 1536), F32),
            pltpu.VMEM((tall, 128), F32),
            pltpu.VMEM((tall, 128), F32),
            pltpu.VMEM((count * 8, 128), F32),
            pltpu.VMEM((count * 8, 128), F32),
            pltpu.VMEM((rows, cols), BF),
            pltpu.VMEM((rows, cols), BF),
            dma((6,)), dma((6,)), dma((6,)), dma((6,)), dma((3,)),
            dma((chips,)), dma((chips,)), dma((chips,)), dma((chips,)), dma((heads,)), dma((heads,)),
        ],
        compiler_params=pltpu.CompilerParams(collective_id=0, has_side_effects=True, vmem_limit_bytes=62 << 20),
    )(step_index, hist_level, feats, conv_weight, conv_bias, lat_weight, noise, hist, w_in, w_hist, gain, k_gain,
      q_gain, live, w_query, w_key, w_value, w_out)


def local(
    feats, conv_weight, conv_bias, latent_projection_weight, noise, step_index, hist, hist_level, hist_count,
    w_in, w_hist, norm_gain, w_query, w_key, w_value, q_gain, k_gain, w_out,
):
    return section(
        step_index, hist_level, feats.transpose(0, 2, 1), conv_weight, conv_bias[None], latent_projection_weight, noise,
        hist, w_in, w_hist.reshape(-1, w_in.shape[1]), norm_gain[None], k_gain[None], q_gain[None], hist_count[None],
        w_query, w_key, w_value, w_out)


def solution(mesh):
    placed = (
        P("seq", None, "grp"), P(), P(), P(), P("seq", None, "grp"), P(), P("seq", None), P("seq"), P(), P(), P(), P(),
        P(None, "grp"), P(None, "grp"), P(None, "grp"), P(), P(), P("grp", None),
    )
    return jax.shard_map(local, mesh=mesh, in_specs=placed, out_specs=P("seq", "grp"), check_vma=False)
```

time: 91.4 us -> 69.9 us (0.76); the launches traced: 90.3 us -> 69.8 us
  Pallas kernels: 88 us -> 67.2 us
    pallas_call x3 -> x1, Pallas kernels: 88 us -> 67.2 us  [section(): pl.pallas_call(section_kernel, out_shape=jax.ShapeDtypeStruct((rows, half...]
where the time goes in v3:
time: 69.9 us; the launch traced here: 69.8 us
  Pallas kernels  67.2 us (96%)
  local copies, waits for them, and re-layouts  1.92 us (3%)
    pallas_call x1, Pallas kernels, section(): pl.pallas_call(section_kernel, out_shape=jax.ShapeDtypeStruct((rows, half...  67.2 us
    unnamed x1, local copies, waits for them, and re-layouts  1.92 us

profile of v3, /device:TPU:4, one launch (start us, length us, event | category | flops | bytes accessed | tf_op | source)
XLA Modules:
  0.0 69.8 jit_solution(10889121517250655609)
XLA Ops:
  0.7 67.2 %shard_map.172 = bf16[192,1536]{1,0:T(8,128)(2,1)} custom-call(s32[1]{0:T(128)S(6)} %copy.20.step_ref, s32[8]{0:T(128)} %level_ref.1, bf16[2,192,128]{2,1,0:T(8,128)(2,1)} %bitcast.8, bf16[3,128,128]{2,1,0:T(8,128)(2,1)} %cw_ref.1, f32[1,128]{1,0:T(1,128)} %bitcast.10, bf16[16,128]{1,0:T(8,128)(2,1)} %lw_ref.1, bf16[2,16,192]{2,1,0:T(8,128)(2,1)} %noise_ref.1, ...), custom_call_target="tpu_custom_call" | custom-call | tf_op jit(solution)/shard_map/pallas_call | solution.py:528
  67.8 1.9 %copy.21 = bf16[192,1536]{1,0:T(8,128)(2,1)} copy(bf16[192,1536]{1,0:T(8,128)(2,1)} %shard_map.172) | data formatting | bytes 1179648

commit v4 on v3

--- a/solution.py
+++ b/solution.py
@@ -85,12 +85,6 @@
         y = (chip + k) % 4
         return (z * 2 + x) * 4 + y
 
-    def back(k):
-        z = (chip // 8 + 4 - (k // 4) % 4) % 4
-        x = (chip // 4 + k // 16) % 2
-        y = (chip + 4 - k % 4) % 4
-        return (z * 2 + x) * 4 + y
-
     cols = kg_ref.shape[1] * 6
     heads = cols // 128
     chunk = 512
@@ -193,6 +187,9 @@
         wide = jnp.where(lane == 64 + head, s * lax.rsqrt(s * s * mean + EPSILON) * (LOG2E / math.sqrt(128.0)), wide)
     hi = wide.astype(BF).astype(F32)
     aux = jnp.where(lane == 80, level, hi + pltpu.roll(wide - hi, 8, 1))
+    owner = lax.broadcasted_iota(jnp.int32, live_ref.shape, 1)
+    live = jnp.sum(jnp.where(owner == seq, live_ref[...].astype(F32), 0.0), axis=1, keepdims=True)
+    aux = jnp.where(lane == 81, jnp.where(line.astype(F32) < live, 1.0, 0.0), aux)
     slots = jnp.concatenate([moved[0:8], aux[0:8]], axis=0)
 
     load_query = pltpu.make_async_copy(wq_hbm, wq_ref, load_sem.at[0])
@@ -266,20 +263,18 @@
     pay_ref[112:128, :] = (c16[:, 128:256] + slots).astype(BF)
     def direct(k):
         return pltpu.make_async_remote_copy(
-            src_ref=pay_ref, dst_ref=g_ref.at[seq], send_sem=send_sem.at[k], recv_sem=recv_sem.at[k],
+            src_ref=pay_ref, dst_ref=g_ref.at[core, k], send_sem=send_sem.at[k], recv_sem=recv_sem.at[k],
             device_id=(grp, shift(k) * 2 + core), device_id_type=MESH)
 
-    def forward(k):
-        source = back(k) * 2 + core
+    def forward(n):
+        lot = g_ref.at[core, pl.ds(n * group, group)]
         return pltpu.make_async_remote_copy(
-            src_ref=g_ref.at[source], dst_ref=g_ref.at[source], send_sem=fsend_sem.at[k], recv_sem=frecv_sem.at[k],
+            src_ref=lot, dst_ref=lot, send_sem=fsend_sem.at[n], recv_sem=frecv_sem.at[n],
             device_id=(grp, sibling), device_id_type=MESH)
-
-    facing = back(plane) * 2 + core
 
     def relay(k):
         return pltpu.make_async_remote_copy(
-            src_ref=g_ref.at[facing], dst_ref=g_ref.at[facing], send_sem=send_sem.at[k], recv_sem=recv_sem.at[k],
+            src_ref=g_ref.at[core, plane], dst_ref=g_ref.at[core, k], send_sem=send_sem.at[k], recv_sem=recv_sem.at[k],
             device_id=(grp, shift(k - plane) * 2 + core), device_id_type=MESH)
 
     direct(plane).start()
@@ -288,10 +283,9 @@
     def _(k):
         direct(k).start()
 
-    here = pltpu.make_async_copy(pay_ref, g_ref.at[seq], load_sem.at[2])
+    here = pltpu.make_async_copy(pay_ref, g_ref.at[core, 0], load_sem.at[2])
     here.start()
     here.wait()
-    forward(0).start()
 
     for j in range(width // chunk):
         part = slice(j * chunk, (j + 1) * chunk)
@@ -305,7 +299,6 @@
     acc[...] = jnp.zeros_like(acc)
     m_ref[...] = jnp.full(m_ref.shape, LOW, F32)
     direct(plane).wait_recv()
-    forward(plane).start()
 
     @pl.loop(plane + 1, chips)
     def _(k):
@@ -329,7 +322,8 @@
     @pl.loop(1, group)
     def _(k):
         direct(k).wait_recv()
-        forward(k).start()
+
+    forward(0).start()
 
     load_query.wait()
     for h in range(heads):
@@ -347,7 +341,8 @@
     @pl.loop(group, 2 * group)
     def _(k):
         direct(k).wait_recv()
-        forward(k).start()
+
+    forward(1).start()
 
     def absorb(h, s):
         sl = slice(h * rows, (h + 1) * rows)
@@ -360,14 +355,12 @@
         return w, jnp.exp2(old - new)
 
     def take(i):
+        forward(i).wait_recv()
         for b in range(0, group, 2):
-            places = []
-            for k in (group * i + b, group * i + b + 1):
-                forward(k).wait_recv()
-                source = back(k) * 2
-                places += [source, source + 1]
             lot = slice(b * 384, b * 384 + 768)
-            unpack([g_ref[place] for place in places], kt.at[:, lot], vt.at[:, lot], cs.at[:, lot])
+            k = group * i + b
+            unpack([g_ref[0, k], g_ref[1, k], g_ref[0, k + 1], g_ref[1, k + 1]],
+                   kt.at[:, lot], vt.at[:, lot], cs.at[:, lot])
 
     def scores(h):
         return jnp.dot(qop[h * rows:(h + 1) * rows, :], kt[...], preferred_element_type=F32)
@@ -391,16 +384,14 @@
         @pl.when((i + 2 < steps) & (i + 2 != steps // 2))
         def _():
             for b in range(group):
-                k = group * (i + 2) + b
-                direct(k).wait_recv()
-                forward(k).start()
+                direct(group * (i + 2) + b).wait_recv()
+            forward(i + 2).start()
 
         @pl.when(i + 2 == steps // 2)
         def _():
             for b in range(1, group):
-                k = plane + b
-                direct(k).wait_recv()
-                forward(k).start()
+                direct(plane + b).wait_recv()
+            forward(i + 2).start()
 
         @pl.when(i == 0)
         def _():
@@ -421,7 +412,7 @@
     @pl.loop(0, chips // 4)
     def _(n):
         for b in range(8):
-            piece = pltpu.roll(g_ref[n * 8 + b, 112:128, :].astype(F32), 64, 1)
+            piece = pltpu.roll(g_ref[n // 4, (n % 4) * 8 + b, 112:128, :].astype(F32), 64, 1)
             spot = pl.ds(pl.multiple_of(n * 64 + b * 8, 8), 8)
             hs[spot, :] = piece[0:8]
             ax[spot, :] = piece[8:16]
@@ -437,12 +428,7 @@
     vh = jnp.concatenate([first * size, jnp.where(lane == 64, 1.0, second * size)], axis=1).astype(BF)
     across = jnp.transpose(ax[...])
     ch = across[0:8] + across[8:16]
-    keys = kh.shape[0]
-    owner = lax.broadcasted_iota(jnp.int32, (keys // 8, keys), 0)
-    slot = lax.broadcasted_iota(jnp.int32, (keys // 8, keys), 1)
-    counts = jnp.dot(jnp.broadcast_to(live_ref[...], (8, keys // 8)).astype(F32).astype(BF),
-                     jnp.where(slot // 8 == owner, 1.0, 0.0).astype(BF), preferred_element_type=F32)
-    hbias = jnp.where((slot[0:1] % 8).astype(F32) < counts[0:1], 0.0, LOW)
+    hbias = jnp.where(across[17:18] > 0.5, 0.0, LOW)
 
     def hist_scores(h):
         sl = slice(h * rows, (h + 1) * rows)
@@ -494,9 +480,9 @@
         out_ref[:, part] = (x_ref[:, part]
                             + jnp.dot(theirs[...], far_ref[:, part], preferred_element_type=F32)).astype(BF)
 
-    @pl.loop(0, chips)
-    def _(k):
-        forward(k).wait_send()
+    @pl.loop(0, steps)
+    def _(n):
+        forward(n).wait_send()
 
     @pl.loop(1, plane + 1)
     def _(k):
@@ -551,7 +537,7 @@
             pltpu.VMEM((2, 128, cols), BF),
             pltpu.VMEM((2, 256, cols), BF),
             pltpu.VMEM((2, 256, cols), BF),
-            pltpu.VMEM((count, 128, 128), BF),
+            pltpu.VMEM((2, chips, 128, 128), BF),
             pltpu.VMEM(w_query.shape, BF),
             pltpu.VMEM((tall, 256), BF),
             pltpu.VMEM((tall, 512), BF),

time: 69.9 us -> 68.3 us (0.977)
  Pallas kernels: 67.2 us -> 65.5 us
    pallas_call x1, Pallas kernels: 67.2 us -> 65.5 us  [section(): pl.pallas_call(section_kernel, out_shape=jax.ShapeDtypeStruct((rows, half...]
where the time goes in v4:
time: 68.3 us; the launch traced here: 68.1 us
  Pallas kernels  65.5 us (96%)
  local copies, waits for them, and re-layouts  1.92 us (3%)
    pallas_call x1, Pallas kernels, section(): pl.pallas_call(section_kernel, out_shape=jax.ShapeDtypeStruct((rows, half...  65.5 us
    unnamed x1, local copies, waits for them, and re-layouts  1.92 us

profile of v4, /device:TPU:4, one launch (start us, length us, event | category | flops | bytes accessed | tf_op | source)
XLA Modules:
  0.0 68.1 jit_solution(17635229727134201935)
XLA Ops:
  0.7 65.5 %shard_map.172 = bf16[192,1536]{1,0:T(8,128)(2,1)} custom-call(s32[1]{0:T(128)S(6)} %copy.20.step_ref, s32[8]{0:T(128)} %level_ref.1, bf16[2,192,128]{2,1,0:T(8,128)(2,1)} %bitcast.8, bf16[3,128,128]{2,1,0:T(8,128)(2,1)} %cw_ref.1, f32[1,128]{1,0:T(1,128)} %bitcast.10, bf16[16,128]{1,0:T(8,128)(2,1)} %lw_ref.1, bf16[2,16,192]{2,1,0:T(8,128)(2,1)} %noise_ref.1, ...), custom_call_target="tpu_custom_call" | custom-call | tf_op jit(solution)/shard_map/pallas_call | solution.py:514
  66.2 1.9 %copy.21 = bf16[192,1536]{1,0:T(8,128)(2,1)} copy(bf16[192,1536]{1,0:T(8,128)(2,1)} %shard_map.172) | data formatting | bytes 1179648
